TPU v7x, 256 devices: a whole 4x4x8 slice. The times are simulated.
256 devices in a mesh: tm: 8 (over x, z_hi), space: 32 (over z_lo, y, core).
Axes of the slice: x: 4, y: 4, z: 8 (z_hi: 2, z_lo: 4; z = z_hi * 4 + z_lo), core: 2. Of those that a mesh axis runs over, the one named last changes fastest.
Arguments:
- orbitals: bfloat16 [13824, 320], P('space'), may hold values from -6 to 6
- gaps: float32 [320], replicated, may hold values from 0.005 to 50
- times: float32 [8], P('tm'), may hold values from 0.01 to 100, as said below
- cos_weights: float32 [8, 8], replicated, may hold values from -1 to 1
Outputs:
- polarizability: float32 [8, 864, 864], P('tm', 'space')
Inputs may be any that keep to these rules, and one draw needn't show every extreme that they name: times rise with their index.
All inputs are finite; a program needn't handle non-finite values.
Results may differ from a plain program's by a relative error of at most 0.0044.
Values may be sent and summed in bfloat16 or wider, within the bound.
A program may use at most 192 MiB of HBM per device.

v0:
```python
import math

import jax
import jax.numpy as jnp
from jax import lax
from jax.sharding import PartitionSpec as P

SIDE = 24
NG = 864
NOCC = 64
NEMP = 256


def plane_table(grid_side, mode_count):
    side_index = jnp.arange(grid_side, dtype=jnp.int32)
    wave_index = jnp.arange(mode_count // 2, dtype=jnp.int32)
    span_first = grid_side // 2
    span_second = grid_side // 4
    wave_first = wave_index % span_first - span_first // 2
    wave_second = wave_index // span_first % span_second - span_second // 2
    wave_third = wave_index // (span_first * span_second) + 1

    def factor(wave_vector):
        step_counts = jnp.mod(wave_vector[:, None] * side_index[None, :], grid_side)
        angles = step_counts.astype(jnp.float32) * (2.0 * math.pi / grid_side)
        return (jnp.cos(angles), jnp.sin(angles))

    cos_first, sin_first = factor(wave_first)
    cos_second, sin_second = factor(wave_second)
    cos_third, sin_third = factor(wave_third)
    cos_first = cos_first[:, :, None, None]
    sin_first = sin_first[:, :, None, None]
    cos_second = cos_second[:, None, :, None]
    sin_second = sin_second[:, None, :, None]
    cos_third = cos_third[:, None, None, :]
    sin_third = sin_third[:, None, None, :]
    inner_cos = cos_second * cos_third - sin_second * sin_third
    inner_sin = sin_second * cos_third + cos_second * sin_third
    cos_whole = cos_first * inner_cos - sin_first * inner_sin
    sin_whole = sin_first * inner_cos + cos_first * inner_sin
    half_count = mode_count // 2
    scaling = math.sqrt(2.0 / grid_side**3)
    joined = jnp.concatenate(
        [cos_whole.reshape(half_count, -1), sin_whole.reshape(half_count, -1)], axis=0
    )
    return (joined * scaling).astype(jnp.bfloat16)


def local(orbitals, gaps, times, cos_weights):
    time_count = times.shape[0]
    table = plane_table(SIDE, NG)
    column_scale = jnp.concatenate(
        [
            jnp.full((NOCC,), NOCC ** (-0.5), jnp.float32),
            jnp.full((NEMP,), NEMP ** (-0.5), jnp.float32),
        ]
    )
    factors = jnp.exp(-gaps[None, :] * times[:, None]) * column_scale[None, :]
    weighted = (orbitals.astype(jnp.float32)[None, :, :] * factors[:, None, :]).astype(jnp.bfloat16)
    row_block = lax.all_gather(orbitals, "space", axis=0, tiled=True)
    green_occ = jnp.einsum(
        "rk,tsk->trs",
        row_block[:, :NOCC],
        weighted[:, :, :NOCC],
        preferred_element_type=jnp.float32,
    )
    green_emp = jnp.einsum(
        "rk,tsk->trs",
        row_block[:, NOCC:],
        weighted[:, :, NOCC:],
        preferred_element_type=jnp.float32,
    )
    chi_block = (green_occ * green_emp).astype(jnp.bfloat16)
    half = jnp.einsum("gr,trs->tgs", table, chi_block, preferred_element_type=jnp.float32)
    half = half.astype(jnp.bfloat16)
    moments = jnp.einsum(
        "tgr,hr->tgh",
        lax.all_to_all(half, "space", split_axis=1, concat_axis=2, tiled=True),
        table,
        preferred_element_type=jnp.float32,
    )
    tm_index = lax.axis_index("tm")
    own_weights = lax.dynamic_slice_in_dim(cos_weights, tm_index * time_count, time_count, 1)
    terms = jnp.einsum("wt,tgh->wgh", own_weights, moments, precision=lax.Precision.HIGHEST)
    result = lax.psum_scatter(terms, "tm", scatter_dimension=0, tiled=True)
    return result


def solution(mesh):
    return jax.shard_map(
        local,
        mesh=mesh,
        in_specs=(P("space", None), P(), P("tm"), P()),
        out_specs=P("tm", "space", None),
        check_vma=False,
    )
```

profile of v0, /device:TPU:6, one launch (start us, length us, event | category | flops | bytes accessed | tf_op | source)
XLA Modules:
  0.0 320.4 jit_solution(17067018593342237799)
XLA Ops:
  6.5 0.0 copy-start
  6.5 0.0 all-gather.3.cloned.1.call-start
  6.5 0.7 all-gather.3.cloned.1.call-update
  8.0 0.7 exponential_multiply_fusion
  8.7 0.2 fusion.32
  8.9 0.4 fusion.24
  9.3 1.1 fusion.14
  10.4 0.3 multiply_subtract_fusion.1
  10.8 19.1 %multiply_subtract_fusion = (f32[432,24,24,24]{0,3,2,1:T(8,128)}, f32[432,24,24,24]{0,3,2,1:T(8,128)}) fusion(f32[432,24,24]{0,2,1:T(8,128)S(1)} %get-tuple-element.8, f32[432,24]{0,1:T(8,128)S(1)} %get-tuple-element.10, f32[432,24,24]{0,2,1:T(8,128)S(1)} %get-tuple-element.7, f32[432,24]{0,1:T(8,128)S(1)} %get-tuple-element.9), kind=kLoop, calls=%fused_computation.3 | loop fusion | flops 35831808 | bytes 49849344 | tf_op jit(solution)/shard_map/sub | solution.py:39
  29.9 54.0 %all-gather.3.cloned.1.call-done = bf16[32,432,320]{1,2,0:T(8,128)(2,1)} async-done(((bf16[1,432,320]{1,2,0:T(8,128)(2,1)}), bf16[32,432,320]{1,2,0:T(8,128)(2,1)}) %all-gather.3.cloned.1.call-update) | async-done | bytes 8847376 | tf_op jit(solution)/shard_map/all_gather | solution.py:60
  83.9 13.9 %copy.8 = bf16[32,432,320]{1,0,2:T(8,128)(2,1)} copy(bf16[32,432,320]{1,2,0:T(8,128)(2,1)} %all-gather.3.cloned.1.call-done) | data formatting | bytes 17694720 | tf_op jit(solution)/shard_map/all_gather | solution.py:60
  97.7 18.0 %reshape.258 = bf16[13824,320]{0,1:T(8,128)(2,1)} reshape(bf16[32,432,320]{1,0,2:T(8,128)(2,1)} %copy.8) | data formatting | bytes 17694720
  115.7 12.7 %fusion.6 = f32[432,13824]{1,0:T(8,128)} fusion(bf16[13824,320]{0,1:T(8,128)(2,1)} %reshape.258, bf16[1,432,320]{1,2,0:T(8,128)(2,1)S(1)} %fusion.14), kind=kOutput, calls=%fused_computation.8 | convolution fusion | flops 764411904 | bytes 25722880 | tf_op jit(solution)/shard_map/rk,tsk->trs/dot_general | solution.py:61
  128.5 29.3 %fusion.11 = bf16[1,864,432]{1,2,0:T(8,128)(2,1)S(1)} fusion(f32[432,13824]{1,0:T(8,128)} %fusion.6, bf16[13824,320]{0,1:T(8,128)(2,1)} %reshape.258, bf16[1,432,320]{1,2,0:T(8,128)(2,1)S(1)} %fusion.14, f32[432,13824]{0,1:T(8,128)} %bitcast.49, f32[432,13824]{0,1:T(8,128)} %bitcast.47), kind=kOutput, calls=%fused_computation.11 | convolution fusion | flops 13425356800 | bytes 88597504 | tf_op jit(solution)/shard_map/gr,trs->tgs/dot_general | solution.py:74
  157.8 2.0 copy.9
  159.8 0.5 broadcast.352
  160.3 6.6 %reduce.4 = bf16[864,432]{1,0:T(8,128)(2,1)S(1)} reduce(bf16[864,1,432]{2,1,0:T(2,128)(2,1)S(1)} %bitcast.51, bf16[]{:T(256)} %broadcast.352), dimensions={1}, to_apply=%bitcast.34.reduce_sub_computation | reduce | bytes 1492994
  166.9 2.7 reshape.261
  169.6 5.2 %all-to-all-start = ((bf16[32,2,5832]{2,1,0:T(2,128)(2,1)}), bf16[32,2,5832]{2,1,0:T(2,128)(2,1)S(1)}, u32[]{:S(2)}, u32[]{:S(2)}) async-start(bf16[32,2,5832]{2,1,0:T(2,128)(2,1)} %reshape.261), calls=%async_computation | async-start | bytes 1507328 | tf_op jit(solution)/shard_map/all_to_all | solution.py:78
  174.8 0.0 reduce-scatter.2.cloned.1.call-start
  174.9 0.0 copy-done
  174.9 0.2 dynamic-slice_reduce_fusion
  175.1 19.8 %all-to-all-done = bf16[32,2,5832]{2,1,0:T(2,128)(2,1)S(1)} async-done(((bf16[32,2,5832]{2,1,0:T(2,128)(2,1)}), bf16[32,2,5832]{2,1,0:T(2,128)(2,1)S(1)}, u32[]{:S(2)}, u32[]{:S(2)}) %all-to-all-start) | async-done | bytes 746528 | tf_op jit(solution)/shard_map/all_to_all | solution.py:78
  194.9 1.7 reshape.262
  196.7 5.0 %bitcast_reduce_fusion = bf16[864,432]{1,0:T(8,128)(2,1)S(1)} fusion(bf16[864,1,432]{2,1,0:T(2,128)(2,1)S(1)} %reshape.262), kind=kLoop, calls=%fused_computation.68 | loop fusion | bytes 1492992 | tf_op jit(solution)/shard_map/all_to_all | solution.py:78
  201.7 0.3 all_to_all.12
  202.1 0.5 copy.10
  202.6 1.5 reshape.256
  204.0 20.1 %fusion.46 = f32[27,864]{1,0:T(8,128)S(1)} fusion(bf16[27,13824]{1,0:T(8,128)(2,1)S(1)} %reshape.256, f32[432,13824]{0,1:T(8,128)} %bitcast.50, f32[432,13824]{0,1:T(8,128)} %bitcast.48), kind=kOutput, calls=%fused_computation.67 | convolution fusion | flops 680804352 | bytes 48615552 | tf_op jit(solution)/shard_map/tgr,hr->tgh/dot_general | solution.py:76
  224.1 1.1 broadcast_multiply_fusion
  225.2 0.0 reduce-scatter.2.cloned.1.call-update
  225.2 86.7 %reduce-scatter.2.cloned.1.call-done = f32[1,27,864]{2,1,0:T(8,128)} async-done(((f32[8,27,864]{2,1,0:T(8,128)}), f32[1,27,864]{2,1,0:T(8,128)}) %reduce-scatter.2.cloned.1.call-update) | async-done | bytes 93328 | tf_op jit(solution)/shard_map/reduce_scatter | solution.py:85
  311.9 1.6 copy.11
  (3 shorter events, 0.0 us)
Async XLA Ops:
  6.5 168.3 %copy-start = (f32[8,8]{1,0:T(8,128)S(1)}, f32[8,8]{1,0:T(8,128)}, u32[]{:S(2)}) copy-start(f32[8,8]{1,0:T(8,128)} %param.7) | copy-start | bytes 772
  6.5 77.3 %all-gather.3.cloned.1.call-start = ((), (), s32[]{:S(2)}) async-start(), calls=%async_computation.3 | async-start | bytes 10813440 | tf_op jit(solution)/shard_map/all_gather | solution.py:60
  169.6 25.3 %all-to-all-start = ((bf16[32,2,5832]{2,1,0:T(2,128)(2,1)}), bf16[32,2,5832]{2,1,0:T(2,128)(2,1)S(1)}, u32[]{:S(2)}, u32[]{:S(2)}) async-start(bf16[32,2,5832]{2,1,0:T(2,128)(2,1)} %reshape.261), calls=%async_computation | async-start | bytes 1507328 | tf_op jit(solution)/shard_map/all_to_all | solution.py:78
  174.8 137.1 %reduce-scatter.2.cloned.1.call-start = ((), (), s32[]{:S(2)}) async-start(), calls=%async_computation.2 | async-start | bytes 1032192 | tf_op jit(solution)/shard_map/reduce_scatter | solution.py:85
Sparse Core Ops, SparseCore 0:
  9.2 74.6 all-gather.2
  225.3 86.5 reduce-scatter.1
where the time goes:
time: 321 us; the launch traced here: 320 us
  waiting for transfers between devices  161 us (50%)
  matrix products  62.1 us (19%)
  local copies, waits for them, and re-layouts  48 us (15%)
  other arithmetic  29.6 us (9%)
  between operations  14.2 us (4%)
  starting transfers between devices  5.24 us (2%)
    reduce_scatter x1, waiting for transfers between devices, local(): result = lax.psum_scatter(terms, 'tm', scatter_dimension=0, tiled=True)  86.7 us
    all_gather x1, waiting for transfers between devices, local(): row_block = lax.all_gather(orbitals, 'space', axis=0, tiled=True)  54 us
    dot_general x1, matrix products, local(): jnp.einsum('gr,trs->tgs', table, chi_block, preferred_element_type=jnp.fl...  29.3 us
    unnamed x6, local copies, waits for them, and re-layouts  23 us
    dot_general x1, matrix products, local(): jnp.einsum('tgr,hr->tgh', lax.all_to_all(half, 'space', split_axis=1, con...  20.1 us
    all_to_all x1, waiting for transfers between devices, local(): lax.all_to_all(half, 'space', split_axis=1, concat_axis=2, tiled=True)  19.8 us
    sub x1, other arithmetic, plane_table(): cos_whole = cos_first * inner_cos - sin_first * inner_sin  19.1 us
    all_gather x1, local copies, waits for them, and re-layouts, local(): row_block = lax.all_gather(orbitals, 'space', axis=0, tiled=True)  13.9 us
  transfers between devices with their start and end apart: 3, of which 3 were waited for; matrix products, arithmetic and copies ran while one was open for 7% of the time, Pallas kernels for 0%

commit v1 on v0

v1 whole, which is shorter than its diff:
```python
import math

import jax
import jax.numpy as jnp
import numpy as np
from jax import lax
from jax.experimental import pallas as pl
from jax.experimental.pallas import tpu as pltpu
from jax.sharding import PartitionSpec as P

SIDE = 24
NG = 864
NOCC = 64
NEMP = 256
MESH = pl.DeviceIdType.MESH
F32 = jnp.float32
BF16 = jnp.bfloat16


def wave_tables():
    pos = np.arange(1024)
    cls, m = pos // 256, pos % 256
    pa, pc = cls >> 1, cls & 1
    trig, ci, bi, ai = m // 108, m // 36 % 3, m // 6 % 6, m % 6
    a, b, c = 2 * ai + pa - 6, bi - 3, 1 + 2 * ci + pc
    valid = m < 216
    natural = np.where(valid, (a + 6) + 12 * (b + 3) + 72 * (c - 1) + 432 * trig, -1)

    def factor(side, wave):
        step = np.mod(side[:, None] * wave[None, :], SIDE)
        angle = step * (2.0 * math.pi / SIDE)
        return np.cos(angle), np.sin(angle)

    x_cos, x_sin = factor(np.arange(16), a)
    y_cos, y_sin = factor(np.arange(24), b)
    y_first = np.where(trig == 0, y_cos, y_sin)
    y_second = np.where(trig == 0, y_sin, -y_cos)
    z_rows = np.concatenate([np.arange(8), np.tile(np.arange(8, 12), 2)])
    z_cos, z_sin = factor(z_rows, c)
    scaling = math.sqrt(2.0 / SIDE**3) * valid
    factors = np.concatenate(
        [x_cos, x_sin, y_first, y_second, z_cos * scaling, z_sin * scaling], axis=0
    ).astype(np.float32)

    where_natural = np.full(1024, -1, np.int32)
    where_natural[natural[valid]] = pos[valid]
    lane = np.arange(1024)
    block, core, low, row = lane // 256, lane // 128 % 2, lane // 32 % 4, lane % 32
    g = 27 * (low * 8 + block * 2 + core) + row
    where_g = np.where(row < 27, where_natural[np.minimum(g, NG - 1)], -1)
    columns = np.stack([where_g, where_natural]).astype(np.int32)

    k = np.arange(256)
    tail = k - 144
    u = np.where(k < 144, k // 8, tail // 8 * 2 + tail % 8 // 4)
    z = np.where(k < 144, k % 8, 8 + tail % 4)
    inside = k < 216
    first = np.where(inside, u * 24 + z, -1)
    second = np.where(inside, u * 24 + 12 + z, -1)
    points = np.concatenate([first, second])[None, :].astype(np.int32)
    return factors, columns, points


FX, FXS, FY, FYS, FZ, FZS = 0, 16, 32, 56, 80, 96


def kernel(
    orb_ref, gaps_ref, times_ref, cw_ref, fac_ref, col_ref, pts_ref, out_ref,
    orb_p, recv, t_own, t_all, lead, quad, table, sel, acc, m_g, m_h, g_all, h_all,
    g_t, dmat, p_buf, keep, c_send, c_recv, q_buf, r_buf,
    a_recv, a_send, t_recv, t_send, g_recv, g_send, h_recv, h_send, l_sem, x_recv, x_send, r_recv, r_send,
):
    tm = lax.axis_index("tm")
    sp = lax.axis_index("space")
    x, zh = tm // 2, tm % 2
    zl, y, core = sp // 8, sp // 2 % 4, sp % 2
    z = zh * 4 + zl

    def device(xx, yy, zz, cc):
        return (xx * 2 + zz // 4, (zz % 4) * 8 + yy * 2 + cc)

    def remote(src, dst, send, recv_sem, target):
        return pltpu.make_async_remote_copy(
            src_ref=src, dst_ref=dst, send_sem=send, recv_sem=recv_sem,
            device_id=target, device_id_type=MESH,
        )

    t_own[...] = jnp.full((8, 128), times_ref[0], F32)
    pick = lax.broadcasted_iota(jnp.int32, (432, 512), 0) == pts_ref[...]
    pick = jnp.where(pick, 1.0, 0.0).astype(BF16)
    moved = jnp.dot(orb_ref[...], pick, preferred_element_type=F32).astype(BF16)
    for n in range(40):
        orb_p[n] = moved[n * 8 : (n + 1) * 8, :]

    for dz, cc in ((2, 0), (-2, 1), (1, 0), (1, 1), (-1, 0), (-1, 1), (0, 0), (0, 1)):
        zz = (z + dz + 8) % 8
        for dy in (2, 1, 3, 0):
            yy = (y + dy) % 4
            blocks = (4 * cc + x, 8 + 4 * zz + yy)
            for part, block in enumerate(blocks):
                src, dst = orb_p.at[block], recv.at[sp, part]
                copy = remote(src, dst, a_send, a_recv, device(x, yy, zz, cc))
                if dz == 0 and dy == 0:
                    local = pltpu.make_async_copy(src, dst, a_recv)
                    pl.when(core == cc)(local.start)
                    pl.when(core != cc)(copy.start)
                else:
                    copy.start()
    for step in range(1, 8):
        remote(t_own, t_all.at[tm], t_send, t_recv, ((tm + step) % 8, sp)).start()
    t_all[tm] = t_own[...]

    def lead_rows(xx, carry):
        cos = fac_ref[pl.ds(FX + xx, 1), :]
        sin = fac_ref[pl.ds(FXS + xx, 1), :]
        first, second = fac_ref[FY : FY + 24, :], fac_ref[FYS : FYS + 24, :]
        rows = pl.ds(pl.multiple_of(xx * 24, 8), 24)
        lead[rows, :] = cos * first - sin * second
        quad[rows, :] = sin * first + cos * second
        return carry

    lax.fori_loop(0, 12, lead_rows, 0)
    odd = lax.broadcasted_iota(jnp.int32, (8, 1024), 0) >= 4

    def table_rows(chunk, carry):
        base = chunk * 18

        def pair(v, inner):
            row = base + 2 * v
            a0, a1 = lead[pl.ds(row, 1), :], lead[pl.ds(row + 1, 1), :]
            b0, b1 = quad[pl.ds(row, 1), :], quad[pl.ds(row + 1, 1), :]
            cos, sin = fac_ref[FZ : FZ + 8, :], fac_ref[FZS : FZS + 8, :]
            both = jnp.concatenate([a0 * cos - b0 * sin, a1 * cos - b1 * sin], axis=0)
            table[chunk, pl.ds(pl.multiple_of(v * 16, 16), 16), :] = both.astype(BF16)
            return inner

        lax.fori_loop(0, 9, pair, 0)

        def tail(v):
            row = base + 2 * v
            a = jnp.where(odd, lead[pl.ds(row + 1, 1), :], lead[pl.ds(row, 1), :])
            b = jnp.where(odd, quad[pl.ds(row + 1, 1), :], quad[pl.ds(row, 1), :])
            return a * fac_ref[FZ + 8 : FZ + 16, :] - b * fac_ref[FZS + 8 : FZS + 16, :]

        def tails(w, inner):
            both = jnp.concatenate([tail(2 * w), tail(jnp.minimum(2 * w + 1, 8))], axis=0)
            table[chunk, pl.ds(pl.multiple_of(144 + w * 16, 16), 16), :] = both.astype(BF16)
            return inner

        lax.fori_loop(0, 5, tails, 0)
        table[chunk, 224:256, :] = jnp.zeros((32, 1024), BF16)
        return carry

    lax.fori_loop(0, 16, table_rows, 0)

    def select_rows(n, carry):
        rows = lax.broadcasted_iota(jnp.int32, (128, 1024), 0) + n * 128
        for side in range(2):
            hit = rows == col_ref[side : side + 1, :]
            sel[side, pl.ds(pl.multiple_of(n * 128, 128), 128), :] = jnp.where(hit, 1.0, 0.0).astype(BF16)
        return carry

    lax.fori_loop(0, 8, select_rows, 0)

    pltpu.make_async_copy(t_all.at[pl.ds(0, 7)], t_all.at[pl.ds(0, 7)], t_recv).wait()
    sub = lax.broadcasted_iota(jnp.int32, (8, 128), 0)
    tcol = jnp.zeros((8, 128), F32)
    for n in range(8):
        tcol = jnp.where(sub == n, t_all[n], tcol)
    tcol = tcol[:, 0:1]
    pair_index = lax.broadcasted_iota(jnp.int32, (1, 1024), 1)
    which_i = 32 * core + 8 * (pair_index // 256) + pair_index // 8 % 8
    which_a = NOCC + 32 * z + 8 * (pair_index // 64 % 4) + pair_index % 8
    orbital = lax.broadcasted_iota(jnp.int32, (320, 1024), 0)
    hot_i = jnp.where(orbital == which_i, 1.0, 0.0).astype(F32)
    hot_a = jnp.where(orbital == which_a, 1.0, 0.0).astype(F32)
    gaps = jnp.broadcast_to(gaps_ref[...], (8, 320))
    high = lax.Precision.HIGHEST
    gap_i = jnp.dot(gaps, hot_i, precision=high, preferred_element_type=F32)
    gap_a = jnp.dot(gaps, hot_a, precision=high, preferred_element_type=F32)
    decay = jnp.exp(-gap_i * tcol) * jnp.exp(-gap_a * tcol) * (NOCC**-0.5 * NEMP**-0.5)
    dmat[...] = jnp.dot(cw_ref[...], decay, precision=high, preferred_element_type=F32)

    acc[...] = jnp.zeros_like(acc)
    pltpu.make_async_copy(recv, recv, a_recv).wait()

    def chunk_step(n, carry):
        i0, e0 = recv[n, 0].astype(F32), recv[n, 1].astype(F32)
        i1, e1 = recv[n + 16, 0].astype(F32), recv[n + 16, 1].astype(F32)
        parts = ([], [], [], [])
        for i in range(8):
            p0, p1 = i0[i : i + 1, :] * e0, i1[i : i + 1, :] * e1
            s, d = p0 + p1, p0 - p1
            parts[0].append(s[:, :256] - s[:, 256:])
            parts[1].append(s[:, :256] + s[:, 256:])
            parts[2].append(d[:, :256] - d[:, 256:])
            parts[3].append(d[:, :256] + d[:, 256:])
        for cls in range(4):
            left = jnp.concatenate(parts[cls], axis=0).astype(BF16)
            lanes = slice(cls * 256, (cls + 1) * 256)
            acc[:, lanes] += jnp.dot(left, table[n, :, lanes], preferred_element_type=F32)
        return carry

    lax.fori_loop(0, 16, chunk_step, 0)
    m_all = acc[...].astype(BF16)
    for n in range(4):
        lanes = slice(n * 256, (n + 1) * 256)
        m_g[n] = jnp.dot(m_all, sel[0, :, lanes], preferred_element_type=F32).astype(BF16)
        m_h[n] = jnp.dot(m_all, sel[1, :, lanes], preferred_element_type=F32).astype(BF16)

    own = x * 4 + y
    for d in (2, 1, 3):
        xx, yy = (x + d) % 4, (y + d) % 4
        remote(m_g.at[xx], g_all.at[own], g_send.at[d], g_recv.at[own], device(xx, y, z, core)).start()
        remote(m_h.at[yy], h_all.at[own], h_send.at[d], h_recv.at[own], device(x, yy, z, core)).start()
    local_g = pltpu.make_async_copy(m_g.at[x], g_all.at[own], g_recv.at[own])
    local_h = pltpu.make_async_copy(m_h.at[y], h_all.at[own], h_recv.at[own])
    local_g.start()
    local_h.start()

    def arrived(buf, sem, slot):
        pltpu.make_async_copy(buf.at[slot], buf.at[slot], sem.at[slot]).wait()

    def pass_g(slot, dy, send):
        remote(g_all.at[slot], g_all.at[slot], g_send.at[send], g_recv.at[slot],
               device(x, (y + dy) % 4, z, core)).start()

    def pass_h(slot, dx, send):
        remote(h_all.at[slot], h_all.at[slot], h_send.at[send], h_recv.at[slot],
               device((x + dx) % 4, y, z, core)).start()

    order = (0, 1, 3, 2)
    for n, d in enumerate(order):
        slot_g, slot_h = (x + d) % 4 * 4 + y, x * 4 + (y + d) % 4
        arrived(g_all, g_recv, slot_g)
        pass_g(slot_g, 1, 4 + 2 * n)
        pass_g(slot_g, 3, 5 + 2 * n)
        arrived(h_all, h_recv, slot_h)
        pass_h(slot_h, 1, 4 + 2 * n)
        pass_h(slot_h, 3, 5 + 2 * n)
    for n, d in enumerate(order):
        up_g, up_h = (x + d) % 4 * 4 + (y + 3) % 4, (x + 3) % 4 * 4 + (y + d) % 4
        down_g, down_h = (x + d) % 4 * 4 + (y + 1) % 4, (x + 1) % 4 * 4 + (y + d) % 4
        arrived(g_all, g_recv, up_g)
        pl.when((x + d) % 4 < 2)(lambda s=up_g, k=12 + n: pass_g(s, 1, k))
        arrived(g_all, g_recv, down_g)
        pl.when((x + d) % 4 >= 2)(lambda s=down_g, k=12 + n: pass_g(s, 3, k))
        arrived(h_all, h_recv, up_h)
        pl.when((y + d) % 4 < 2)(lambda s=up_h, k=12 + n: pass_h(s, 1, k))
        arrived(h_all, h_recv, down_h)
        pl.when((y + d) % 4 >= 2)(lambda s=down_h, k=12 + n: pass_h(s, 3, k))
    for d in range(4):
        arrived(g_all, g_recv, d * 4 + (y + 2) % 4)
        arrived(h_all, h_recv, (x + 2) % 4 * 4 + d)

    for n in range(8):
        rows = slice(n * 128, (n + 1) * 128)
        block = jnp.concatenate([g_all[2 * n], g_all[2 * n + 1]], axis=0).astype(F32)
        g_t[:, rows] = block.T
    sibling = device(x, y, z, 1 - core)
    mine = pl.ds(pl.multiple_of(core * 128, 128), 128)
    other = pl.ds(pl.multiple_of((1 - core) * 128, 128), 128)

    def frequency(w, carry):
        total = jnp.zeros((256, 256), F32)
        for n in range(4):
            lanes = slice(n * 256, (n + 1) * 256)
            left = (g_t[:, lanes] * dmat[pl.ds(w, 1), lanes]).astype(BF16)
            right = h_all[4 * n : 4 * n + 4].reshape(256, 256)
            total += jnp.dot(left, right, preferred_element_type=F32)
        p_buf[...] = total
        keep[w] = p_buf[mine, :]
        c_send[w] = p_buf[other, :].astype(BF16)
        remote(c_send.at[w], c_recv.at[w], x_send.at[w], x_recv.at[w], sibling).start()
        return carry

    lax.fori_loop(0, 8, frequency, 0)

    slot = z * 4 + y

    def deliver(w, carry):
        pltpu.make_async_copy(c_recv.at[w], c_recv.at[w], x_recv.at[w]).wait()
        total = (keep[w] + c_recv[w].astype(F32)).astype(BF16)
        for low in range(4):
            q_buf[w * 4 + low] = total[low * 32 : (low + 1) * 32, :]
        for low in range(4):
            src = q_buf.at[w * 4 + low]
            target = low * 8 + x * 2 + core
            copy = remote(src, r_buf.at[slot], r_send, r_recv, (w, target))
            local = pltpu.make_async_copy(src, r_buf.at[slot], r_recv)
            here = jnp.logical_and(w == tm, target == sp)
            pl.when(here)(local.start)
            pl.when(jnp.logical_not(here))(copy.start)
        return carry

    lax.fori_loop(0, 8, deliver, 0)
    pltpu.make_async_copy(r_buf, r_buf, r_recv).wait()
    for n in range(4):
        total = r_buf[n].astype(F32)
        for m in range(1, 8):
            total += r_buf[m * 4 + n].astype(F32)
        width = 256 if n < 3 else 96
        out_ref[:, n * 256 : n * 256 + width] = total[:27, :width]

    away = jnp.where(jnp.logical_and(x == y, True), 1, 0)
    pltpu.make_async_copy(recv.at[pl.ds(0, 31)], recv.at[pl.ds(0, 31)], a_send).wait()
    pltpu.make_async_copy(t_all.at[pl.ds(0, 7)], t_all.at[pl.ds(0, 7)], t_send).wait()
    for n in range(1, 16):
        pltpu.make_async_copy(m_g.at[0], m_g.at[0], g_send.at[n]).wait()
        pltpu.make_async_copy(m_h.at[0], m_h.at[0], h_send.at[n]).wait()
    for n in range(8):
        pltpu.make_async_copy(c_send.at[n], c_send.at[n], x_send.at[n]).wait()
    short = pltpu.make_async_copy(q_buf.at[pl.ds(0, 31)], q_buf.at[pl.ds(0, 31)], r_send)
    whole = pltpu.make_async_copy(q_buf, q_buf, r_send)
    pl.when(away == 1)(short.wait)
    pl.when(away == 0)(whole.wait)


def local(orbitals, gaps, times, cos_weights):
    factors, columns, points = wave_tables()
    vmem = pl.BlockSpec(memory_space=pltpu.VMEM)
    smem = pl.BlockSpec(memory_space=pltpu.SMEM)
    dma = pltpu.SemaphoreType.DMA
    out = pl.pallas_call(
        kernel,
        out_shape=jax.ShapeDtypeStruct((27, NG), F32),
        in_specs=[vmem, vmem, smem, vmem, vmem, vmem, vmem],
        out_specs=vmem,
        scratch_shapes=[
            pltpu.VMEM((40, 8, 512), BF16),
            pltpu.VMEM((32, 2, 8, 512), BF16),
            pltpu.VMEM((8, 128), F32),
            pltpu.VMEM((8, 8, 128), F32),
            pltpu.VMEM((288, 1024), F32),
            pltpu.VMEM((288, 1024), F32),
            pltpu.VMEM((16, 256, 1024), BF16),
            pltpu.VMEM((2, 1024, 1024), BF16),
            pltpu.VMEM((64, 1024), F32),
            pltpu.VMEM((4, 64, 256), BF16),
            pltpu.VMEM((4, 64, 256), BF16),
            pltpu.VMEM((16, 64, 256), BF16),
            pltpu.VMEM((16, 64, 256), BF16),
            pltpu.VMEM((256, 1024), F32),
            pltpu.VMEM((8, 1024), F32),
            pltpu.VMEM((256, 256), F32),
            pltpu.VMEM((8, 128, 256), F32),
            pltpu.VMEM((8, 128, 256), BF16),
            pltpu.VMEM((8, 128, 256), BF16),
            pltpu.VMEM((32, 32, 256), BF16),
            pltpu.VMEM((32, 32, 256), BF16),
            dma, dma, dma, dma,
            dma((16,)), dma((16,)), dma((16,)), dma((16,)),
            dma,
            dma((8,)), dma((8,)),
            dma, dma,
        ],
        compiler_params=pltpu.CompilerParams(has_side_effects=True),
    )(
        orbitals.T, gaps[None, :], times, cos_weights,
        jnp.asarray(factors), jnp.asarray(columns), jnp.asarray(points),
    )
    return out[None]


def solution(mesh):
    return jax.shard_map(
        local,
        mesh=mesh,
        in_specs=(P("space", None), P(), P("tm"), P()),
        out_specs=P("tm", "space", None),
        check_vma=False,
    )
```

time: 321 us -> 69.1 us (0.22)
  waiting for transfers between devices: 161 us -> 0 us
  Pallas kernels: 0 us -> 66.1 us
  matrix products: 62.1 us -> 0 us
  local copies, waits for them, and re-layouts: 48 us -> 2.22 us
  other arithmetic: 29.6 us -> 0 us
  between operations: 14.2 us -> 0.68 us
  starting transfers between devices: 5.24 us -> 0 us
    reduce_scatter x1 -> x0, waiting for transfers between devices: 86.7 us -> none  [local(): result = lax.psum_scatter(terms, 'tm', scatter_dimension=0, tiled=True)]
    pallas_call x0 -> x1, Pallas kernels: none -> 66.1 us  [local(): pl.pallas_call(kernel, out_shape=jax.ShapeDtypeStruct((27, NG), F32), in_...]
    dot_general x3 -> x0, matrix products: 62.1 us -> none  [the longest x1 29.3 us: local(): jnp.einsum('gr,trs->tgs', table, chi_block, preferred_element_type=jnp.fl...]
    all_gather x1 -> x0, waiting for transfers between devices: 54 us -> none  [local(): row_block = lax.all_gather(orbitals, 'space', axis=0, tiled=True)]
    unnamed x6 -> x2, local copies, waits for them, and re-layouts: 23 us -> 0.02 us
    all_to_all x1 -> x0, waiting for transfers between devices: 19.8 us -> none  [local(): lax.all_to_all(half, 'space', split_axis=1, concat_axis=2, tiled=True)]
    sub x4 -> x0, other arithmetic: 19.5 us -> none  [the longest x1 19.1 us: plane_table(): cos_whole = cos_first * inner_cos - sin_first * inner_sin]
    all_gather x1 -> x0, local copies, waits for them, and re-layouts: 13.9 us -> none  [local(): row_block = lax.all_gather(orbitals, 'space', axis=0, tiled=True)]
  transfers between devices with their start and end apart: 3 -> 0, of which waited for: 3 -> 0; matrix products, arithmetic and copies ran while one was open for 7% -> 0% of each run, Pallas kernels for 0% -> 0%
where the time goes in v1:
time: 69.1 us; the launch traced here: 69 us
  Pallas kernels  66.1 us (96%)
  local copies, waits for them, and re-layouts  2.22 us (3%)
    pallas_call x1, Pallas kernels, local(): pl.pallas_call(kernel, out_shape=jax.ShapeDtypeStruct((27, NG), F32), in_...  66.1 us
    broadcast_in_dim x1, local copies, waits for them, and re-layouts, local(): return out[None]  1.64 us

profile of v1, /device:TPU:6, one launch (start us, length us, event | category | flops | bytes accessed | tf_op | source)
XLA Modules:
  0.0 69.0 jit_solution(7959476793501515902)
XLA Ops:
  0.0 0.0 copy-start
  0.7 0.0 copy-done
  0.7 0.6 broadcast_in_dim.6.gaps_ref
  1.2 66.1 %shard_map.73 = f32[27,864]{1,0:T(8,128)} custom-call(bf16[320,432]{1,0:T(8,128)(2,1)} %bitcast.3, f32[1,320]{1,0:T(1,128)} %broadcast_in_dim.6.gaps_ref, f32[1]{0:T(128)S(6)} %copy.9.times_ref, f32[8,8]{1,0:T(8,128)} %cw_ref.1, f32[112,1024]{1,0:T(8,128)} %constant.6.clone.fac_ref, s32[2,1024]{1,0:T(2,128)} %constant.7.clone.col_ref, ...), custom_call_target="tpu_custom_call" | custom-call | tf_op jit(solution)/shard_map/pallas_call | solution.py:324
  67.4 1.6 %copy.8 = f32[1,27,864]{2,0,1:T(1,128)} copy(f32[1,27,864]{2,1,0:T(8,128)} %bitcast.2) | data formatting | bytes 186624 | tf_op jit(solution)/shard_map/broadcast_in_dim | solution.py:362
Async XLA Ops:
  0.0 0.7 copy-start

commit v2 on v1

--- a/solution.py
+++ b/solution.py
@@ -66,7 +66,7 @@
 
 def kernel(
     orb_ref, gaps_ref, times_ref, cw_ref, fac_ref, col_ref, pts_ref, out_ref,
-    orb_p, recv, t_own, t_all, lead, quad, table, sel, acc, m_g, m_h, g_all, h_all,
+    orb_p, recv, t_own, t_all, lead, quad, table, sel, gap_i, gap_a, acc, m_g, m_h, g_all, h_all,
     g_t, dmat, p_buf, keep, c_send, c_recv, q_buf, r_buf,
     a_recv, a_send, t_recv, t_send, g_recv, g_send, h_recv, h_send, l_sem, x_recv, x_send, r_recv, r_send,
 ):
@@ -85,6 +85,25 @@
             device_id=target, device_id_type=MESH,
         )
 
+    barrier = pltpu.get_barrier_semaphore()
+
+    def greet(target):
+        pl.semaphore_signal(barrier, inc=1, device_id=target, device_id_type=MESH)
+
+    far = (z + 6 + 4 * core) % 8
+    for dy in (2, 1, 3, 0):
+        yy = (y + dy) % 4
+        for cc in range(2):
+            greet(device(x, yy, far, cc))
+            greet(device(x, yy, (z + 1) % 8, cc))
+            greet(device(x, yy, (z + 7) % 8, cc))
+        if dy > 0:
+            greet(device(x, yy, z, core))
+        greet(device(x, yy, z, 1 - core))
+    for dx in range(1, 4):
+        greet(device((x + dx) % 4, y, z, core))
+    greet(device(x, y, (z + 4) % 8, core))
+
     t_own[...] = jnp.full((8, 128), times_ref[0], F32)
     pick = lax.broadcasted_iota(jnp.int32, (432, 512), 0) == pts_ref[...]
     pick = jnp.where(pick, 1.0, 0.0).astype(BF16)
@@ -92,6 +111,7 @@
     for n in range(40):
         orb_p[n] = moved[n * 8 : (n + 1) * 8, :]
 
+    pl.semaphore_wait(barrier, 35)
     for dz, cc in ((2, 0), (-2, 1), (1, 0), (1, 1), (-1, 0), (-1, 1), (0, 0), (0, 1)):
         zz = (z + dz + 8) % 8
         for dy in (2, 1, 3, 0):
@@ -99,15 +119,13 @@
             blocks = (4 * cc + x, 8 + 4 * zz + yy)
             for part, block in enumerate(blocks):
                 src, dst = orb_p.at[block], recv.at[sp, part]
-                copy = remote(src, dst, a_send, a_recv, device(x, yy, zz, cc))
+                copy = remote(src, dst, a_send, a_recv.at[sp], device(x, yy, zz, cc))
                 if dz == 0 and dy == 0:
-                    local = pltpu.make_async_copy(src, dst, a_recv)
+                    local = pltpu.make_async_copy(src, dst, a_recv.at[sp])
                     pl.when(core == cc)(local.start)
                     pl.when(core != cc)(copy.start)
                 else:
                     copy.start()
-    for step in range(1, 8):
-        remote(t_own, t_all.at[tm], t_send, t_recv, ((tm + step) % 8, sp)).start()
     t_all[tm] = t_own[...]
 
     def lead_rows(xx, carry):
@@ -162,12 +180,6 @@
 
     lax.fori_loop(0, 8, select_rows, 0)
 
-    pltpu.make_async_copy(t_all.at[pl.ds(0, 7)], t_all.at[pl.ds(0, 7)], t_recv).wait()
-    sub = lax.broadcasted_iota(jnp.int32, (8, 128), 0)
-    tcol = jnp.zeros((8, 128), F32)
-    for n in range(8):
-        tcol = jnp.where(sub == n, t_all[n], tcol)
-    tcol = tcol[:, 0:1]
     pair_index = lax.broadcasted_iota(jnp.int32, (1, 1024), 1)
     which_i = 32 * core + 8 * (pair_index // 256) + pair_index // 8 % 8
     which_a = NOCC + 32 * z + 8 * (pair_index // 64 % 4) + pair_index % 8
@@ -176,15 +188,16 @@
     hot_a = jnp.where(orbital == which_a, 1.0, 0.0).astype(F32)
     gaps = jnp.broadcast_to(gaps_ref[...], (8, 320))
     high = lax.Precision.HIGHEST
-    gap_i = jnp.dot(gaps, hot_i, precision=high, preferred_element_type=F32)
-    gap_a = jnp.dot(gaps, hot_a, precision=high, preferred_element_type=F32)
-    decay = jnp.exp(-gap_i * tcol) * jnp.exp(-gap_a * tcol) * (NOCC**-0.5 * NEMP**-0.5)
-    dmat[...] = jnp.dot(cw_ref[...], decay, precision=high, preferred_element_type=F32)
+    gap_i[...] = jnp.dot(gaps, hot_i, precision=high, preferred_element_type=F32)
+    gap_a[...] = jnp.dot(gaps, hot_a, precision=high, preferred_element_type=F32)
 
     acc[...] = jnp.zeros_like(acc)
-    pltpu.make_async_copy(recv, recv, a_recv).wait()
-
-    def chunk_step(n, carry):
+
+    def chunk_step(step, carry):
+        low = jnp.where(step < 8, 1 - zl % 2, zl % 2)
+        n = low * 8 + (step % 8 + 2 * y) % 8
+        for shard in (n, n + 16):
+            pltpu.make_async_copy(recv.at[shard], recv.at[shard], a_recv.at[shard]).wait()
         i0, e0 = recv[n, 0].astype(F32), recv[n, 1].astype(F32)
         i1, e1 = recv[n + 16, 0].astype(F32), recv[n + 16, 1].astype(F32)
         parts = ([], [], [], [])
@@ -213,10 +226,12 @@
         xx, yy = (x + d) % 4, (y + d) % 4
         remote(m_g.at[xx], g_all.at[own], g_send.at[d], g_recv.at[own], device(xx, y, z, core)).start()
         remote(m_h.at[yy], h_all.at[own], h_send.at[d], h_recv.at[own], device(x, yy, z, core)).start()
-    local_g = pltpu.make_async_copy(m_g.at[x], g_all.at[own], g_recv.at[own])
-    local_h = pltpu.make_async_copy(m_h.at[y], h_all.at[own], h_recv.at[own])
-    local_g.start()
-    local_h.start()
+    for n, d in enumerate((1, 3)):
+        yy, xx = (y + d) % 4, (x + d) % 4
+        remote(m_g.at[x], g_all.at[own], g_send.at[4 + n], g_recv.at[own], device(x, yy, z, core)).start()
+        remote(m_h.at[y], h_all.at[own], h_send.at[4 + n], h_recv.at[own], device(xx, y, z, core)).start()
+    pltpu.make_async_copy(m_g.at[x], g_all.at[own], g_recv.at[own]).start()
+    pltpu.make_async_copy(m_h.at[y], h_all.at[own], h_recv.at[own]).start()
 
     def arrived(buf, sem, slot):
         pltpu.make_async_copy(buf.at[slot], buf.at[slot], sem.at[slot]).wait()
@@ -231,6 +246,8 @@
 
     order = (0, 1, 3, 2)
     for n, d in enumerate(order):
+        if d == 0:
+            continue
         slot_g, slot_h = (x + d) % 4 * 4 + y, x * 4 + (y + d) % 4
         arrived(g_all, g_recv, slot_g)
         pass_g(slot_g, 1, 4 + 2 * n)
@@ -238,6 +255,8 @@
         arrived(h_all, h_recv, slot_h)
         pass_h(slot_h, 1, 4 + 2 * n)
         pass_h(slot_h, 3, 5 + 2 * n)
+    for step in range(1, 8):
+        remote(t_own, t_all.at[tm], t_send, t_recv, ((tm + step) % 8, sp)).start()
     for n, d in enumerate(order):
         up_g, up_h = (x + d) % 4 * 4 + (y + 3) % 4, (x + 3) % 4 * 4 + (y + d) % 4
         down_g, down_h = (x + d) % 4 * 4 + (y + 1) % 4, (x + 1) % 4 * 4 + (y + d) % 4
@@ -249,6 +268,17 @@
         pl.when((y + d) % 4 < 2)(lambda s=up_h, k=12 + n: pass_h(s, 1, k))
         arrived(h_all, h_recv, down_h)
         pl.when((y + d) % 4 >= 2)(lambda s=down_h, k=12 + n: pass_h(s, 3, k))
+    arrived(g_all, g_recv, own)
+    arrived(h_all, h_recv, own)
+
+    pltpu.make_async_copy(t_all.at[pl.ds(0, 7)], t_all.at[pl.ds(0, 7)], t_recv).wait()
+    sub = lax.broadcasted_iota(jnp.int32, (8, 128), 0)
+    tcol = jnp.zeros((8, 128), F32)
+    for n in range(8):
+        tcol = jnp.where(sub == n, t_all[n], tcol)
+    tcol = tcol[:, 0:1]
+    decay = jnp.exp(-gap_i[...] * tcol) * jnp.exp(-gap_a[...] * tcol) * (NOCC**-0.5 * NEMP**-0.5)
+    dmat[...] = jnp.dot(cw_ref[...], decay, precision=high, preferred_element_type=F32)
     for d in range(4):
         arrived(g_all, g_recv, d * 4 + (y + 2) % 4)
         arrived(h_all, h_recv, (x + 2) % 4 * 4 + d)
@@ -261,24 +291,9 @@
     mine = pl.ds(pl.multiple_of(core * 128, 128), 128)
     other = pl.ds(pl.multiple_of((1 - core) * 128, 128), 128)
 
-    def frequency(w, carry):
-        total = jnp.zeros((256, 256), F32)
-        for n in range(4):
-            lanes = slice(n * 256, (n + 1) * 256)
-            left = (g_t[:, lanes] * dmat[pl.ds(w, 1), lanes]).astype(BF16)
-            right = h_all[4 * n : 4 * n + 4].reshape(256, 256)
-            total += jnp.dot(left, right, preferred_element_type=F32)
-        p_buf[...] = total
-        keep[w] = p_buf[mine, :]
-        c_send[w] = p_buf[other, :].astype(BF16)
-        remote(c_send.at[w], c_recv.at[w], x_send.at[w], x_recv.at[w], sibling).start()
-        return carry
-
-    lax.fori_loop(0, 8, frequency, 0)
-
     slot = z * 4 + y
 
-    def deliver(w, carry):
+    def deliver(w):
         pltpu.make_async_copy(c_recv.at[w], c_recv.at[w], x_recv.at[w]).wait()
         total = (keep[w] + c_recv[w].astype(F32)).astype(BF16)
         for low in range(4):
@@ -291,9 +306,23 @@
             here = jnp.logical_and(w == tm, target == sp)
             pl.when(here)(local.start)
             pl.when(jnp.logical_not(here))(copy.start)
+
+    def frequency(w, carry):
+        total = jnp.zeros((256, 256), F32)
+        for n in range(4):
+            lanes = slice(n * 256, (n + 1) * 256)
+            left = (g_t[:, lanes] * dmat[pl.ds(w, 1), lanes]).astype(BF16)
+            right = h_all[4 * n : 4 * n + 4].reshape(256, 256)
+            total += jnp.dot(left, right, preferred_element_type=F32)
+        p_buf[...] = total
+        keep[w] = p_buf[mine, :]
+        c_send[w] = p_buf[other, :].astype(BF16)
+        remote(c_send.at[w], c_recv.at[w], x_send.at[w], x_recv.at[w], sibling).start()
+        pl.when(w >= 4)(lambda: deliver(w - 4))
         return carry
 
-    lax.fori_loop(0, 8, deliver, 0)
+    lax.fori_loop(0, 8, frequency, 0)
+    lax.fori_loop(4, 8, lambda w, carry: (deliver(w), carry)[1], 0)
     pltpu.make_async_copy(r_buf, r_buf, r_recv).wait()
     for n in range(4):
         total = r_buf[n].astype(F32)
@@ -335,6 +364,8 @@
             pltpu.VMEM((288, 1024), F32),
             pltpu.VMEM((16, 256, 1024), BF16),
             pltpu.VMEM((2, 1024, 1024), BF16),
+            pltpu.VMEM((8, 1024), F32),
+            pltpu.VMEM((8, 1024), F32),
             pltpu.VMEM((64, 1024), F32),
             pltpu.VMEM((4, 64, 256), BF16),
             pltpu.VMEM((4, 64, 256), BF16),
@@ -348,13 +379,13 @@
             pltpu.VMEM((8, 128, 256), BF16),
             pltpu.VMEM((32, 32, 256), BF16),
             pltpu.VMEM((32, 32, 256), BF16),
-            dma, dma, dma, dma,
+            dma((32,)), dma, dma, dma,
             dma((16,)), dma((16,)), dma((16,)), dma((16,)),
             dma,
             dma((8,)), dma((8,)),
             dma, dma,
         ],
-        compiler_params=pltpu.CompilerParams(has_side_effects=True),
+        compiler_params=pltpu.CompilerParams(has_side_effects=True, collective_id=0),
     )(
         orbitals.T, gaps[None, :], times, cos_weights,
         jnp.asarray(factors), jnp.asarray(columns), jnp.asarray(points),

time: 69.1 us -> 57.5 us (0.83)
  Pallas kernels: 66.1 us -> 54.4 us
    pallas_call x1, Pallas kernels: 66.1 us -> 54.4 us  [local(): pl.pallas_call(kernel, out_shape=jax.ShapeDtypeStruct((27, NG), F32), in_...]
where the time goes in v2:
time: 57.5 us; the launch traced here: 57.3 us
  Pallas kernels  54.4 us (95%)
  local copies, waits for them, and re-layouts  2.22 us (4%)
  between operations  0.68 us (1%)
    pallas_call x1, Pallas kernels, local(): pl.pallas_call(kernel, out_shape=jax.ShapeDtypeStruct((27, NG), F32), in_...  54.4 us
    broadcast_in_dim x1, local copies, waits for them, and re-layouts, local(): return out[None]  1.64 us

profile of v2, /device:TPU:6, one launch (start us, length us, event | category | flops | bytes accessed | tf_op | source)
XLA Modules:
  0.0 57.3 jit_solution(5886523538771110496)
XLA Ops:
  0.0 0.0 copy-start
  0.7 0.0 copy-done
  0.7 0.6 broadcast_in_dim.6.gaps_ref
  1.2 54.4 %shard_map.73 = f32[27,864]{1,0:T(8,128)} custom-call(bf16[320,432]{1,0:T(8,128)(2,1)} %bitcast.3, f32[1,320]{1,0:T(1,128)} %broadcast_in_dim.6.gaps_ref, f32[1]{0:T(128)S(6)} %copy.9.times_ref, f32[8,8]{1,0:T(8,128)} %cw_ref.1, f32[112,1024]{1,0:T(8,128)} %constant.6.clone.fac_ref, s32[2,1024]{1,0:T(2,128)} %constant.7.clone.col_ref, ...), custom_call_target="tpu_custom_call" | custom-call | tf_op jit(solution)/shard_map/pallas_call | solution.py:353
  55.7 1.6 %copy.8 = f32[1,27,864]{2,0,1:T(1,128)} copy(f32[1,27,864]{2,1,0:T(8,128)} %bitcast.2) | data formatting | bytes 186624 | tf_op jit(solution)/shard_map/broadcast_in_dim | solution.py:393
Async XLA Ops:
  0.0 0.7 %copy-start = (f32[320]{0:T(512)S(1)}, f32[320]{0:T(512)}, u32[]{:S(2)}) copy-start(f32[320]{0:T(512)} %param.8) | copy-start | bytes 3844

commit v3 on v2

v3 whole, which is shorter than its diff:
```python
import math

import jax
import jax.numpy as jnp
import numpy as np
from jax import lax
from jax.experimental import pallas as pl
from jax.experimental.pallas import tpu as pltpu
from jax.sharding import PartitionSpec as P

SIDE = 24
NG = 864
NOCC = 64
NEMP = 256
MESH = pl.DeviceIdType.MESH
F32 = jnp.float32
BF16 = jnp.bfloat16


def wave_tables():
    pos = np.arange(1024)
    group, m = pos // 128, pos % 128
    even = group < 4
    c_even = np.where(even, group % 2, (group - 4) // 2)
    trig = np.where(even, m // 54, group % 2)
    c = 1 + 2 * np.where(even, m // 18 % 3, m // 36) + c_even
    b = np.where(even, m // 3, m // 6) % 6 - 3
    a = np.where(even, 4 * (m % 3) - 4 - 2 * (group // 2), 2 * (m % 6) - 5)
    valid = m < 108
    natural = np.where(valid, (a + 6) + 12 * (b + 3) + 72 * (c - 1) + 432 * trig, -1)

    def factor(side, wave):
        step = np.mod(side[:, None] * wave[None, :], SIDE)
        angle = step * (2.0 * math.pi / SIDE)
        return np.cos(angle), np.sin(angle)

    x_cos, x_sin = factor(np.arange(8), a)
    y_cos, y_sin = factor(np.arange(24), b)
    y_first = np.where(trig == 0, y_cos, y_sin)
    y_second = np.where(trig == 0, y_sin, -y_cos)
    z_rows = np.concatenate([np.arange(8), np.tile(np.arange(8, 12), 2)])
    z_cos, z_sin = factor(z_rows, c)
    scaling = math.sqrt(2.0 / SIDE**3) * valid
    turn = np.where(a % 4 == 1, 1.0, -1.0) * np.ones((8, 1))
    factors = np.concatenate(
        [x_cos, x_sin, y_first, y_second, z_cos * scaling, z_sin * scaling, turn], axis=0
    ).astype(np.float32)

    where_natural = np.full(1024, -1, np.int32)
    where_natural[natural[valid]] = pos[valid]
    lane = np.arange(1024)
    block, core, low, row = lane // 256, lane // 128 % 2, lane // 32 % 4, lane % 32
    g = 27 * (low * 8 + block * 2 + core) + row
    where_g = np.where(row < 27, where_natural[np.minimum(g, NG - 1)], -1)
    offsets = np.repeat(np.array(OFFSETS), 64, axis=0).T
    columns = np.stack([where_g, where_natural, offsets[0], offsets[1]]).astype(np.int32)

    k = np.arange(256)
    tail = k - 144
    u = np.where(k < 144, k // 8, tail // 8 * 2 + tail % 8 // 4)
    z = np.where(k < 144, k % 8, 8 + tail % 4)
    inside = k < 216
    first = np.where(inside, u * 24 + z, -1)
    second = np.where(inside, u * 24 + 12 + z, -1)
    points = np.concatenate([first, second])[None, :].astype(np.int32)
    return factors, columns, points


OFFSETS = (
    (0, 0), (0, 1), (0, 3), (1, 0), (3, 0), (1, 1), (3, 3), (1, 3),
    (3, 1), (0, 2), (2, 0), (1, 2), (2, 1), (3, 2), (2, 3), (2, 2),
)
SLOT = {offset: n for n, offset in enumerate(OFFSETS)}
FX, FXS, FY, FYS, FZ, FZS, FT = 0, 8, 16, 40, 64, 80, 96


def kernel(
    orb_hbm, gaps_hbm, times_hbm, cw_hbm, fac_hbm, col_hbm, pts_hbm, out_any,
    out_ref, gaps_ref, times_ref, cw_ref, col_ref, pts_ref, orb_ref, fac_ref,
    orb_p, recv, t_own, t_all, lead, quad, table, sel, acc, acc_odd, m_g, m_h, g_all, h_all,
    g_t, dmat, both, keep, c_send, c_recv, q_buf, s_buf, f_buf, r_buf,
    a_recv, a_send, t_recv, t_send, u_recv, u_send, g_recv, g_send, h_recv, h_send, l_sem, x_recv, x_send, s_recv, s_send, r_recv, r_send,
):
    tm = lax.axis_index("tm")
    sp = lax.axis_index("space")
    x, zh = tm // 2, tm % 2
    zl, y, core = sp // 8, sp // 2 % 4, sp % 2
    z = zh * 4 + zl

    def device(xx, yy, zz, cc):
        return (xx * 2 + zz // 4, (zz % 4) * 8 + yy * 2 + cc)

    def remote(src, dst, send, recv_sem, target):
        return pltpu.make_async_remote_copy(
            src_ref=src, dst_ref=dst, send_sem=send, recv_sem=recv_sem,
            device_id=target, device_id_type=MESH,
        )

    barrier = pltpu.get_barrier_semaphore()

    def greet(target):
        pl.semaphore_signal(barrier, inc=1, device_id=target, device_id_type=MESH)

    far = (z + 6 + 4 * core) % 8
    for dy in (2, 1, 3, 0):
        yy = (y + dy) % 4
        for cc in range(2):
            greet(device(x, yy, far, cc))
            greet(device(x, yy, (z + 1) % 8, cc))
            greet(device(x, yy, (z + 7) % 8, cc))
        if dy > 0:
            greet(device(x, yy, z, core))
        greet(device(x, yy, z, 1 - core))
    for dx in range(1, 4):
        greet(device((x + dx) % 4, y, z, core))
    greet(device(x, y, (z + 4) % 8, core))

    load_orb = pltpu.make_async_copy(orb_hbm, orb_ref, l_sem.at[0])
    load_pts = pltpu.make_async_copy(pts_hbm, pts_ref, l_sem.at[1])
    load_orb.start()
    load_pts.start()
    loads = [
        pltpu.make_async_copy(src, dst, l_sem.at[2 + n])
        for n, (src, dst) in enumerate((
            (fac_hbm, fac_ref), (col_hbm, col_ref), (gaps_hbm, gaps_ref), (cw_hbm, cw_ref), (times_hbm, times_ref),
        ))
    ]
    for load in loads:
        load.start()

    load_pts.wait()
    pick = lax.broadcasted_iota(jnp.int32, (432, 512), 0) == pts_ref[...]
    pick = jnp.where(pick, 1.0, 0.0).astype(BF16)
    load_orb.wait()
    moved = jnp.dot(orb_ref[...], pick, preferred_element_type=F32).astype(BF16)
    for n in range(40):
        orb_p[n] = moved[n * 8 : (n + 1) * 8, :]

    pl.semaphore_wait(barrier, 35)
    for dy in (2, 1, 3, 0):
        yy = (y + dy) % 4
        for dz, cc in ((2, 0), (-2, 1), (1, 0), (-1, 1), (1, 1), (-1, 0), (0, 0), (0, 1)):
            zz = (z + dz + 8) % 8
            blocks = (4 * cc + x, 8 + 4 * zz + yy)
            for part, block in enumerate(blocks):
                src, dst = orb_p.at[block], recv.at[sp, part]
                copy = remote(src, dst, a_send, a_recv.at[sp], device(x, yy, zz, cc))
                if dz == 0 and dy == 0:
                    local = pltpu.make_async_copy(src, dst, a_recv.at[sp])
                    pl.when(core == cc)(local.start)
                    pl.when(core != cc)(copy.start)
                else:
                    copy.start()
    for load in loads:
        load.wait()
    t_own[...] = jnp.full((8, 128), times_ref[0], F32)
    for dx in range(1, 4):
        remote(t_own, t_all.at[zh * 4 + x], t_send, t_recv, device((x + dx) % 4, y, z, core)).start()
    t_all[zh * 4 + x] = t_own[...]

    def lead_rows(xx, carry):
        cos = fac_ref[pl.ds(FX + xx, 1), :]
        sin = fac_ref[pl.ds(FXS + xx, 1), :]
        first, second = fac_ref[FY : FY + 24, :], fac_ref[FYS : FYS + 24, :]
        rows = pl.ds(pl.multiple_of(xx * 24, 8), 24)
        lead[rows, :] = cos * first - sin * second
        quad[rows, :] = sin * first + cos * second
        return carry

    lax.fori_loop(0, 6, lead_rows, 0)
    odd = lax.broadcasted_iota(jnp.int32, (8, 1024), 0) >= 4

    def table_rows(chunk, carry):
        base = chunk * 18

        def pair(v, inner):
            row = base + 2 * v
            a0, a1 = lead[pl.ds(row, 1), :], lead[pl.ds(row + 1, 1), :]
            b0, b1 = quad[pl.ds(row, 1), :], quad[pl.ds(row + 1, 1), :]
            cos, sin = fac_ref[FZ : FZ + 8, :], fac_ref[FZS : FZS + 8, :]
            both = jnp.concatenate([a0 * cos - b0 * sin, a1 * cos - b1 * sin], axis=0)
            table[chunk, pl.ds(pl.multiple_of(v * 16, 16), 16), :] = both.astype(BF16)
            return inner

        lax.fori_loop(0, 9, pair, 0)

        def tail(v):
            row = base + 2 * v
            a = jnp.where(odd, lead[pl.ds(row + 1, 1), :], lead[pl.ds(row, 1), :])
            b = jnp.where(odd, quad[pl.ds(row + 1, 1), :], quad[pl.ds(row, 1), :])
            return a * fac_ref[FZ + 8 : FZ + 16, :] - b * fac_ref[FZS + 8 : FZS + 16, :]

        def tails(w, inner):
            both = jnp.concatenate([tail(2 * w), tail(jnp.minimum(2 * w + 1, 8))], axis=0)
            table[chunk, pl.ds(pl.multiple_of(144 + w * 16, 16), 16), :] = both.astype(BF16)
            return inner

        lax.fori_loop(0, 5, tails, 0)
        table[chunk, 224:256, :] = jnp.zeros((32, 1024), BF16)
        return carry

    lax.fori_loop(0, 8, table_rows, 0)

    def select_rows(n, carry):
        rows = lax.broadcasted_iota(jnp.int32, (128, 1024), 0) + n * 128
        for side in range(2):
            hit = rows == col_ref[side : side + 1, :]
            sel[side, pl.ds(pl.multiple_of(n * 128, 128), 128), :] = jnp.where(hit, 1.0, 0.0).astype(BF16)
        return carry

    lax.fori_loop(0, 8, select_rows, 0)

    pltpu.make_async_copy(t_all.at[pl.ds(0, 3)], t_all.at[pl.ds(0, 3)], t_recv).wait()
    half_times = t_all.at[pl.ds(zh * 4, 4)]
    remote(half_times, half_times, u_send, u_recv, device(x, y, (z + 4) % 8, core)).start()

    acc[...] = jnp.zeros_like(acc)
    acc_odd[...] = jnp.zeros_like(acc_odd)

    def chunk_step(step, carry):
        turn = step // 2
        away = jnp.where(turn == 0, 2, 2 * turn - 1)
        away = jnp.where(turn == 3, 0, away)
        n = (y + away) % 4 * 2 + step % 2
        for quarter in range(4):
            shard = n + 8 * quarter
            pltpu.make_async_copy(recv.at[shard], recv.at[shard], a_recv.at[shard]).wait()
        occupied = [recv[n + 8 * quarter, 0].astype(F32) for quarter in range(4)]
        empty = [recv[n + 8 * quarter, 1].astype(F32) for quarter in range(4)]
        minus, plus = ([], [], [], []), ([], [], [], [])
        for i in range(8):
            p = [o[i : i + 1, :] * e for o, e in zip(occupied, empty)]
            s0, s1, d0, d1 = p[0] + p[2], p[1] + p[3], p[0] - p[2], p[1] - p[3]
            for kind, value in enumerate((s0 + s1, s0 - s1, d0, d1)):
                minus[kind].append(value[:, :256] - value[:, 256:])
                plus[kind].append(value[:, :256] + value[:, 256:])

        def product(rows, start, width):
            left = jnp.concatenate(rows, axis=0).astype(BF16)
            return jnp.dot(left, table[n, :, start : start + width], preferred_element_type=F32)

        acc[:, 0:128] += product(minus[0], 0, 128)
        acc[:, 128:256] += product(plus[0], 128, 128)
        acc[:, 256:384] += product(minus[1], 256, 128)
        acc[:, 384:512] += product(plus[1], 384, 128)
        acc_odd[:, 0:256] += product(minus[2] + minus[3], 512, 256)
        acc_odd[:, 256:512] += product(plus[2] + plus[3], 768, 256)
        return carry

    lax.fori_loop(0, 8, chunk_step, 0)
    columns = [acc[...]]
    for part in range(2):
        at = part * 256
        sign = fac_ref[FT : FT + 1, 512 + at : 640 + at]
        u_cos, u_sin = acc_odd[0:64, at : at + 128], acc_odd[0:64, at + 128 : at + 256]
        v_cos, v_sin = acc_odd[64:128, at : at + 128], acc_odd[64:128, at + 128 : at + 256]
        columns += [u_cos - sign * v_sin, u_sin + sign * v_cos]
    m_all = jnp.concatenate(columns, axis=1).astype(BF16)
    for n in range(4):
        lanes = slice(n * 256, (n + 1) * 256)
        m_g[n] = jnp.dot(m_all, sel[0, :, lanes], preferred_element_type=F32).astype(BF16)
        m_h[n] = jnp.dot(m_all, sel[1, :, lanes], preferred_element_type=F32).astype(BF16)

    def send_g(src, to, dx, dy, send):
        target = device((x + dx) % 4, (y + dy) % 4, z, core)
        remote(src, g_all.at[to], g_send.at[send], g_recv.at[to], target).start()

    def send_h(src, to, dx, dy, send):
        target = device((x + dx) % 4, (y + dy) % 4, z, core)
        remote(src, h_all.at[to], h_send.at[send], h_recv.at[to], target).start()

    for d in (2, 1, 3):
        send_g(m_g.at[(y + d) % 4], SLOT[0, 4 - d], 0, d, d)
        send_h(m_h.at[(x + d) % 4], SLOT[4 - d, 0], d, 0, d)
    for n, d in enumerate((1, 3)):
        send_g(m_g.at[y], SLOT[4 - d, 0], d, 0, 4 + n)
        send_h(m_h.at[x], SLOT[0, 4 - d], 0, d, 4 + n)
    pltpu.make_async_copy(m_g.at[y], g_all.at[0], g_recv.at[0]).start()
    pltpu.make_async_copy(m_h.at[x], h_all.at[0], h_recv.at[0]).start()

    pltpu.make_async_copy(half_times, half_times, u_recv).wait()
    pair_index = lax.broadcasted_iota(jnp.int32, (1, 1024), 1)
    which_i = 32 * core + 8 * ((col_ref[2:3, :] + x) % 4) + pair_index // 8 % 8
    which_a = NOCC + 32 * z + 8 * ((col_ref[3:4, :] + y) % 4) + pair_index % 8
    orbital = lax.broadcasted_iota(jnp.int32, (320, 1024), 0)
    hot_i = jnp.where(orbital == which_i, 1.0, 0.0).astype(F32)
    hot_a = jnp.where(orbital == which_a, 1.0, 0.0).astype(F32)
    gaps = jnp.broadcast_to(gaps_ref[...].reshape(1, 320), (8, 320))
    high = lax.Precision.HIGHEST
    gap_i = jnp.dot(gaps, hot_i, precision=high, preferred_element_type=F32)
    gap_a = jnp.dot(gaps, hot_a, precision=high, preferred_element_type=F32)
    sub = lax.broadcasted_iota(jnp.int32, (8, 128), 0)
    tcol = jnp.zeros((8, 128), F32)
    for n in range(8):
        tcol = jnp.where(sub == n, t_all[n % 2 * 4 + n // 2], tcol)
    tcol = tcol[:, 0:1]
    decay = jnp.exp(-gap_i * tcol) * jnp.exp(-gap_a * tcol) * (NOCC**-0.5 * NEMP**-0.5)
    dmat[...] = jnp.dot(cw_ref[...], decay, precision=high, preferred_element_type=F32)

    def arrived(buf, sem, slot):
        pltpu.make_async_copy(buf.at[slot], buf.at[slot], sem.at[slot]).wait()

    def got_g(dx, dy):
        arrived(g_all, g_recv, SLOT[dx, dy])

    def got_h(dx, dy):
        arrived(h_all, h_recv, SLOT[dx, dy])

    def relay(d, n):
        got_g(3, d)
        up = (y + d) % 4 < 2
        pl.when(up)(lambda: send_g(g_all.at[SLOT[3, d]], SLOT[2, d], 1, 0, 12 + n))
        got_g(1, d)
        pl.when(jnp.logical_not(up))(lambda: send_g(g_all.at[SLOT[1, d]], SLOT[2, d], 3, 0, 12 + n))
        got_h(d, 3)
        up = (x + d) % 4 < 2
        pl.when(up)(lambda: send_h(h_all.at[SLOT[d, 3]], SLOT[d, 2], 0, 1, 12 + n))
        got_h(d, 1)
        pl.when(jnp.logical_not(up))(lambda: send_h(h_all.at[SLOT[d, 1]], SLOT[d, 2], 0, 3, 12 + n))

    relay(0, 0)
    for n, d in enumerate((1, 3, 2)):
        got_g(0, d)
        send_g(g_all.at[SLOT[0, d]], SLOT[3, d], 1, 0, 6 + 2 * n)
        send_g(g_all.at[SLOT[0, d]], SLOT[1, d], 3, 0, 7 + 2 * n)
        got_h(d, 0)
        send_h(h_all.at[SLOT[d, 0]], SLOT[d, 3], 0, 1, 6 + 2 * n)
        send_h(h_all.at[SLOT[d, 0]], SLOT[d, 1], 0, 3, 7 + 2 * n)
    for n, d in enumerate((1, 3, 2)):
        relay(d, 1 + n)
    got_g(0, 0)
    got_h(0, 0)

    def turn_g(start):
        for n in range(start, start + 4):
            block = jnp.concatenate([g_all[2 * n], g_all[2 * n + 1]], axis=0).astype(F32)
            g_t[:, n * 128 : (n + 1) * 128] = block.T

    turn_g(0)
    h_early = h_all[0:8].reshape(512, 256)

    def early(w, carry):
        left = (g_t[:, 0:512] * dmat[pl.ds(w, 1), 0:512]).astype(BF16)
        keep[w] = jnp.dot(left, h_early, preferred_element_type=F32)
        return carry

    lax.fori_loop(0, 8, early, 0)
    for d in range(4):
        got_g(2, d)
        got_h(d, 2)
    turn_g(4)
    sibling = device(x, y, z, 1 - core)
    mine = pl.ds(pl.multiple_of(core * 128, 128), 128)
    other = pl.ds(pl.multiple_of((1 - core) * 128, 128), 128)

    side = 2 * ((z + core) % 2) - 1
    partner = device(x, y, (z - side + 8) % 8, core)

    h_late = h_all[8:16].reshape(512, 256)

    def late(w, rows):
        left = [g_t[rows, 512:1024] * dmat[pl.ds(w + n, 1), 512:1024] for n in range(2)]
        left = jnp.concatenate(left, axis=0).astype(BF16)
        return jnp.dot(left, h_late, preferred_element_type=F32)

    def for_sibling(n, carry):
        total = late(2 * n, other)
        for m in range(2):
            w = 2 * n + m
            c_send[w] = (keep[w, other, :] + total[m * 128 : (m + 1) * 128, :]).astype(BF16)
            remote(c_send.at[w], c_recv.at[w], x_send.at[w], x_recv.at[w], sibling).start()
        return carry

    def both_cores(n, carry):
        rest = late(2 * n, mine)
        for m in range(2):
            w = 2 * n + m
            pltpu.make_async_copy(c_recv.at[w], c_recv.at[w], x_recv.at[w]).wait()
            total = keep[w, mine, :] + rest[m * 128 : (m + 1) * 128, :] + c_recv[w].astype(F32)
            both[w] = total
            for low in range(4):
                q_buf[w * 4 + low] = total[low * 32 : (low + 1) * 32, :].astype(BF16)
            for low in range(4):
                owner = m * 4 + low
                step = ((owner - z) * side + 8) % 8
                there = n * 4 + 7 - step
                copy = remote(q_buf.at[w * 4 + low], s_buf.at[there], s_send, s_recv.at[there], partner)
                pl.when(step >= 4)(copy.start)
        return carry

    lax.fori_loop(0, 4, for_sibling, 0)
    lax.fori_loop(0, 4, both_cores, 0)
    slot = (z + core) // 2 % 4 * 4 + x

    def deliver(n, carry):
        step = 3 - n % 4
        owner = (z + side * step + 8) % 8
        w, low = n // 4 * 2 + owner // 4, owner % 4
        here = n // 4 * 4 + step
        pltpu.make_async_copy(s_buf.at[here], s_buf.at[here], s_recv.at[here]).wait()
        rows = pl.ds(pl.multiple_of(low * 32, 32), 32)
        f_buf[here] = (both[w, rows, :] + s_buf[here].astype(F32)).astype(BF16)
        target = low * 8 + y * 2 + core
        copy = remote(f_buf.at[here], r_buf.at[slot], r_send, r_recv, (w, target))
        local = pltpu.make_async_copy(f_buf.at[here], r_buf.at[slot], r_recv)
        own_block = jnp.logical_and(w == tm, target == sp)
        pl.when(own_block)(local.start)
        pl.when(jnp.logical_not(own_block))(copy.start)
        return carry

    lax.fori_loop(0, 16, deliver, 0)
    pltpu.make_async_copy(r_buf, r_buf, r_recv).wait()
    for n in range(4):
        total = r_buf[n].astype(F32)
        for m in range(1, 4):
            total += r_buf[m * 4 + n].astype(F32)
        width = 256 if n < 3 else 96
        out_ref[:, 0, n * 256 : n * 256 + width] = total[:27, :width]

    final = pltpu.make_async_copy(out_ref, out_any, l_sem.at[0])
    final.start()

    pltpu.make_async_copy(recv.at[pl.ds(0, 31)], recv.at[pl.ds(0, 31)], a_send).wait()
    pltpu.make_async_copy(t_all.at[pl.ds(0, 3)], t_all.at[pl.ds(0, 3)], t_send).wait()
    pltpu.make_async_copy(half_times, half_times, u_send).wait()
    for n in range(1, 16):
        pltpu.make_async_copy(m_g.at[0], m_g.at[0], g_send.at[n]).wait()
        pltpu.make_async_copy(m_h.at[0], m_h.at[0], h_send.at[n]).wait()
    for n in range(8):
        pltpu.make_async_copy(c_send.at[n], c_send.at[n], x_send.at[n]).wait()
    pltpu.make_async_copy(s_buf, s_buf, s_send).wait()
    final.wait()
    pltpu.make_async_copy(f_buf.at[pl.ds(0, 15)], f_buf.at[pl.ds(0, 15)], r_send).wait()


def local(orbitals, gaps, times, cos_weights):
    factors, columns, points = wave_tables()
    stay = lambda value: pltpu.with_memory_space_constraint(value, pltpu.HBM)
    dma = pltpu.SemaphoreType.DMA
    out = pl.pallas_call(
        kernel,
        out_shape=jax.ShapeDtypeStruct((27, 1, NG), F32),
        in_specs=[pl.BlockSpec(memory_space=pltpu.HBM)] * 7,
        out_specs=pl.BlockSpec(memory_space=pl.ANY),
        scratch_shapes=[
            pltpu.VMEM((27, 1, NG), F32),
            pltpu.VMEM((NOCC + NEMP,), F32),
            pltpu.SMEM((1,), F32),
            pltpu.VMEM((8, 8), F32),
            pltpu.VMEM((4, 1024), jnp.int32),
            pltpu.VMEM((1, 512), jnp.int32),
            pltpu.VMEM((320, 432), BF16),
            pltpu.VMEM((104, 1024), F32),
            pltpu.VMEM((40, 8, 512), BF16),
            pltpu.VMEM((32, 2, 8, 512), BF16),
            pltpu.VMEM((8, 128), F32),
            pltpu.VMEM((8, 8, 128), F32),
            pltpu.VMEM((144, 1024), F32),
            pltpu.VMEM((144, 1024), F32),
            pltpu.VMEM((8, 256, 1024), BF16),
            pltpu.VMEM((2, 1024, 1024), BF16),
            pltpu.VMEM((64, 512), F32),
            pltpu.VMEM((128, 512), F32),
            pltpu.VMEM((4, 64, 256), BF16),
            pltpu.VMEM((4, 64, 256), BF16),
            pltpu.VMEM((16, 64, 256), BF16),
            pltpu.VMEM((16, 64, 256), BF16),
            pltpu.VMEM((256, 1024), F32),
            pltpu.VMEM((8, 1024), F32),
            pltpu.VMEM((8, 128, 256), F32),
            pltpu.VMEM((8, 256, 256), F32),
            pltpu.VMEM((8, 128, 256), BF16),
            pltpu.VMEM((8, 128, 256), BF16),
            pltpu.VMEM((32, 32, 256), BF16),
            pltpu.VMEM((16, 32, 256), BF16),
            pltpu.VMEM((16, 32, 256), BF16),
            pltpu.VMEM((16, 32, 256), BF16),
            dma((32,)), dma, dma, dma, dma, dma,
            dma((16,)), dma((16,)), dma((16,)), dma((16,)),
            dma((7,)),
            dma((8,)), dma((8,)),
            dma((16,)), dma,
            dma, dma,
        ],
        compiler_params=pltpu.CompilerParams(has_side_effects=True, collective_id=0, vmem_limit_bytes=34 * 2**20),
    )(
        stay(orbitals.T), stay(gaps), times, stay(cos_weights),
        stay(jnp.asarray(factors)), stay(jnp.asarray(columns)), stay(jnp.asarray(points)),
    )
    return out.transpose(1, 0, 2)


def solution(mesh):
    return jax.shard_map(
        local,
        mesh=mesh,
        in_specs=(P("space", None), P(), P("tm"), P()),
        out_specs=P("tm", "space", None),
        check_vma=False,
    )
```

time: 57.5 us -> 50.3 us (0.87)
  Pallas kernels: 54.4 us -> 48.9 us
  local copies, waits for them, and re-layouts: 2.22 us -> 0.64 us
    pallas_call x1, Pallas kernels: 54.4 us -> 48.9 us  [local(): pl.pallas_call(kernel, out_shape=jax.ShapeDtypeStruct((27, 1, NG), F32),...]
    broadcast_in_dim x2 -> x0, local copies, waits for them, and re-layouts: 2.2 us -> none  [the longest x1 1.64 us: local(): return out[None]]
    unnamed x2 -> x1, local copies, waits for them, and re-layouts: 0.02 us -> 0.64 us
where the time goes in v3:
time: 50.3 us; the launch traced here: 50.2 us
  Pallas kernels  48.9 us (97%)
  between operations  0.66 us (1%)
  local copies, waits for them, and re-layouts  0.64 us (1%)
    pallas_call x1, Pallas kernels, local(): pl.pallas_call(kernel, out_shape=jax.ShapeDtypeStruct((27, 1, NG), F32),...  48.9 us

profile of v3, /device:TPU:6, one launch (start us, length us, event | category | flops | bytes accessed | tf_op | source)
XLA Modules:
  0.0 50.2 jit_solution(4151527938353142905)
XLA Ops:
  0.7 48.9 %shard_map.73 = f32[27,1,864]{2,1,0:T(1,128)S(1)} custom-call(bf16[320,432]{1,0:T(8,128)(2,1)} %bitcast.3, f32[320]{0:T(512)} %gaps_hbm.1, f32[1]{0:T(128)S(6)} %copy.9.times_hbm, f32[8,8]{1,0:T(8,128)} %cw_hbm.1, f32[104,1024]{1,0:T(8,128)} %constant.6.clone.fac_hbm, s32[4,1024]{1,0:T(4,128)} %constant.7.clone.col_hbm, s32[1,512]{1,0:T(1,128)} %constant.8.clone.pts_hbm), custom_call_target="tpu_custom_call" | custom-call | tf_op jit(solution)/shard_map/pallas_call | solution.py:440
  49.6 0.6 %copy.10 = f32[1,27,864]{2,0,1:T(1,128)} copy(f32[1,27,864]{2,0,1:T(1,128)S(1)} %bitcast.2) | data formatting | bytes 186624

commit v4 on v3

--- a/solution.py
+++ b/solution.py
@@ -95,6 +95,19 @@
             src_ref=src, dst_ref=dst, send_sem=send, recv_sem=recv_sem,
             device_id=target, device_id_type=MESH,
         )
+
+    load_orb = pltpu.make_async_copy(orb_hbm, orb_ref, l_sem.at[0])
+    load_pts = pltpu.make_async_copy(pts_hbm, pts_ref, l_sem.at[1])
+    load_orb.start()
+    load_pts.start()
+    loads = [
+        pltpu.make_async_copy(src, dst, l_sem.at[2])
+        for n, (src, dst) in enumerate((
+            (fac_hbm, fac_ref), (col_hbm, col_ref), (gaps_hbm, gaps_ref), (cw_hbm, cw_ref), (times_hbm, times_ref),
+        ))
+    ]
+    for load in loads:
+        load.start()
 
     barrier = pltpu.get_barrier_semaphore()
 
@@ -115,19 +128,6 @@
         greet(device((x + dx) % 4, y, z, core))
     greet(device(x, y, (z + 4) % 8, core))
 
-    load_orb = pltpu.make_async_copy(orb_hbm, orb_ref, l_sem.at[0])
-    load_pts = pltpu.make_async_copy(pts_hbm, pts_ref, l_sem.at[1])
-    load_orb.start()
-    load_pts.start()
-    loads = [
-        pltpu.make_async_copy(src, dst, l_sem.at[2 + n])
-        for n, (src, dst) in enumerate((
-            (fac_hbm, fac_ref), (col_hbm, col_ref), (gaps_hbm, gaps_ref), (cw_hbm, cw_ref), (times_hbm, times_ref),
-        ))
-    ]
-    for load in loads:
-        load.start()
-
     load_pts.wait()
     pick = lax.broadcasted_iota(jnp.int32, (432, 512), 0) == pts_ref[...]
     pick = jnp.where(pick, 1.0, 0.0).astype(BF16)
@@ -137,20 +137,19 @@
         orb_p[n] = moved[n * 8 : (n + 1) * 8, :]
 
     pl.semaphore_wait(barrier, 35)
-    for dy in (2, 1, 3, 0):
-        yy = (y + dy) % 4
-        for dz, cc in ((2, 0), (-2, 1), (1, 0), (-1, 1), (1, 1), (-1, 0), (0, 0), (0, 1)):
-            zz = (z + dz + 8) % 8
-            blocks = (4 * cc + x, 8 + 4 * zz + yy)
-            for part, block in enumerate(blocks):
-                src, dst = orb_p.at[block], recv.at[sp, part]
-                copy = remote(src, dst, a_send, a_recv.at[sp], device(x, yy, zz, cc))
-                if dz == 0 and dy == 0:
-                    local = pltpu.make_async_copy(src, dst, a_recv.at[sp])
-                    pl.when(core == cc)(local.start)
-                    pl.when(core != cc)(copy.start)
-                else:
-                    copy.start()
+    links = ((2, 0), (-2, 1), (1, 0), (-1, 1), (1, 1), (-1, 0), (0, 0), (0, 1))
+    for dy, (dz, cc) in [(dy, link) for pair in ((1, 3), (2, 0)) for link in links for dy in pair]:
+        yy, zz = (y + dy) % 4, (z + dz + 8) % 8
+        blocks = (4 * cc + x, 8 + 4 * zz + yy)
+        for part, block in enumerate(blocks):
+            src, dst = orb_p.at[block], recv.at[sp, part]
+            copy = remote(src, dst, a_send, a_recv.at[sp % 8], device(x, yy, zz, cc))
+            if dz == 0 and dy == 0:
+                local = pltpu.make_async_copy(src, dst, a_recv.at[sp % 8])
+                pl.when(core == cc)(local.start)
+                pl.when(core != cc)(copy.start)
+            else:
+                copy.start()
     for load in loads:
         load.wait()
     t_own[...] = jnp.full((8, 128), times_ref[0], F32)
@@ -219,12 +218,9 @@
 
     def chunk_step(step, carry):
         turn = step // 2
-        away = jnp.where(turn == 0, 2, 2 * turn - 1)
-        away = jnp.where(turn == 3, 0, away)
+        away = jnp.where(turn < 2, 2 * turn + 1, 6 - 2 * turn)
         n = (y + away) % 4 * 2 + step % 2
-        for quarter in range(4):
-            shard = n + 8 * quarter
-            pltpu.make_async_copy(recv.at[shard], recv.at[shard], a_recv.at[shard]).wait()
+        pltpu.make_async_copy(recv.at[pl.ds(0, 4)], recv.at[pl.ds(0, 4)], a_recv.at[n]).wait()
         occupied = [recv[n + 8 * quarter, 0].astype(F32) for quarter in range(4)]
         empty = [recv[n + 8 * quarter, 1].astype(F32) for quarter in range(4)]
         minus, plus = ([], [], [], []), ([], [], [], [])
@@ -261,20 +257,20 @@
         m_g[n] = jnp.dot(m_all, sel[0, :, lanes], preferred_element_type=F32).astype(BF16)
         m_h[n] = jnp.dot(m_all, sel[1, :, lanes], preferred_element_type=F32).astype(BF16)
 
-    def send_g(src, to, dx, dy, send):
+    def send_g(src, to, dx, dy):
         target = device((x + dx) % 4, (y + dy) % 4, z, core)
-        remote(src, g_all.at[to], g_send.at[send], g_recv.at[to], target).start()
-
-    def send_h(src, to, dx, dy, send):
+        remote(src, g_all.at[to], g_send, g_recv.at[to], target).start()
+
+    def send_h(src, to, dx, dy):
         target = device((x + dx) % 4, (y + dy) % 4, z, core)
-        remote(src, h_all.at[to], h_send.at[send], h_recv.at[to], target).start()
+        remote(src, h_all.at[to], h_send, h_recv.at[to], target).start()
 
     for d in (2, 1, 3):
-        send_g(m_g.at[(y + d) % 4], SLOT[0, 4 - d], 0, d, d)
-        send_h(m_h.at[(x + d) % 4], SLOT[4 - d, 0], d, 0, d)
-    for n, d in enumerate((1, 3)):
-        send_g(m_g.at[y], SLOT[4 - d, 0], d, 0, 4 + n)
-        send_h(m_h.at[x], SLOT[0, 4 - d], 0, d, 4 + n)
+        send_g(m_g.at[(y + d) % 4], SLOT[0, 4 - d], 0, d)
+        send_h(m_h.at[(x + d) % 4], SLOT[4 - d, 0], d, 0)
+    for d in (1, 3):
+        send_g(m_g.at[y], SLOT[4 - d, 0], d, 0)
+        send_h(m_h.at[x], SLOT[0, 4 - d], 0, d)
     pltpu.make_async_copy(m_g.at[y], g_all.at[0], g_recv.at[0]).start()
     pltpu.make_async_copy(m_h.at[x], h_all.at[0], h_recv.at[0]).start()
 
@@ -306,28 +302,29 @@
     def got_h(dx, dy):
         arrived(h_all, h_recv, SLOT[dx, dy])
 
-    def relay(d, n):
+    def relay(d):
         got_g(3, d)
         up = (y + d) % 4 < 2
-        pl.when(up)(lambda: send_g(g_all.at[SLOT[3, d]], SLOT[2, d], 1, 0, 12 + n))
+        pl.when(up)(lambda: send_g(g_all.at[SLOT[3, d]], SLOT[2, d], 1, 0))
         got_g(1, d)
-        pl.when(jnp.logical_not(up))(lambda: send_g(g_all.at[SLOT[1, d]], SLOT[2, d], 3, 0, 12 + n))
+        pl.when(jnp.logical_not(up))(lambda: send_g(g_all.at[SLOT[1, d]], SLOT[2, d], 3, 0))
         got_h(d, 3)
         up = (x + d) % 4 < 2
-        pl.when(up)(lambda: send_h(h_all.at[SLOT[d, 3]], SLOT[d, 2], 0, 1, 12 + n))
+        pl.when(up)(lambda: send_h(h_all.at[SLOT[d, 3]], SLOT[d, 2], 0, 1))
         got_h(d, 1)
-        pl.when(jnp.logical_not(up))(lambda: send_h(h_all.at[SLOT[d, 1]], SLOT[d, 2], 0, 3, 12 + n))
-
-    relay(0, 0)
-    for n, d in enumerate((1, 3, 2)):
+        pl.when(jnp.logical_not(up))(lambda: send_h(h_all.at[SLOT[d, 1]], SLOT[d, 2], 0, 3))
+
+    relay(0)
+    for d in (1, 3, 2):
         got_g(0, d)
-        send_g(g_all.at[SLOT[0, d]], SLOT[3, d], 1, 0, 6 + 2 * n)
-        send_g(g_all.at[SLOT[0, d]], SLOT[1, d], 3, 0, 7 + 2 * n)
+        send_g(g_all.at[SLOT[0, d]], SLOT[3, d], 1, 0)
+        send_g(g_all.at[SLOT[0, d]], SLOT[1, d], 3, 0)
         got_h(d, 0)
-        send_h(h_all.at[SLOT[d, 0]], SLOT[d, 3], 0, 1, 6 + 2 * n)
-        send_h(h_all.at[SLOT[d, 0]], SLOT[d, 1], 0, 3, 7 + 2 * n)
-    for n, d in enumerate((1, 3, 2)):
-        relay(d, 1 + n)
+        send_h(h_all.at[SLOT[d, 0]], SLOT[d, 3], 0, 1)
+        send_h(h_all.at[SLOT[d, 0]], SLOT[d, 1], 0, 3)
+    relay(1)
+    relay(3)
+    relay(2)
     got_g(0, 0)
     got_h(0, 0)
 
@@ -364,17 +361,19 @@
         return jnp.dot(left, h_late, preferred_element_type=F32)
 
     def for_sibling(n, carry):
-        total = late(2 * n, other)
+        first = 2 * n
+        total = late(first, other)
         for m in range(2):
-            w = 2 * n + m
+            w = first + m
             c_send[w] = (keep[w, other, :] + total[m * 128 : (m + 1) * 128, :]).astype(BF16)
-            remote(c_send.at[w], c_recv.at[w], x_send.at[w], x_recv.at[w], sibling).start()
+            remote(c_send.at[w], c_recv.at[w], x_send, x_recv.at[w], sibling).start()
         return carry
 
     def both_cores(n, carry):
-        rest = late(2 * n, mine)
+        first = 2 * n
+        rest = late(first, mine)
         for m in range(2):
-            w = 2 * n + m
+            w = first + m
             pltpu.make_async_copy(c_recv.at[w], c_recv.at[w], x_recv.at[w]).wait()
             total = keep[w, mine, :] + rest[m * 128 : (m + 1) * 128, :] + c_recv[w].astype(F32)
             both[w] = total
@@ -383,7 +382,7 @@
             for low in range(4):
                 owner = m * 4 + low
                 step = ((owner - z) * side + 8) % 8
-                there = n * 4 + 7 - step
+                there = first * 2 + 7 - step
                 copy = remote(q_buf.at[w * 4 + low], s_buf.at[there], s_send, s_recv.at[there], partner)
                 pl.when(step >= 4)(copy.start)
         return carry
@@ -395,8 +394,9 @@
     def deliver(n, carry):
         step = 3 - n % 4
         owner = (z + side * step + 8) % 8
-        w, low = n // 4 * 2 + owner // 4, owner % 4
-        here = n // 4 * 4 + step
+        pair = n // 4
+        w, low = pair * 2 + owner // 4, owner % 4
+        here = pair * 4 + step
         pltpu.make_async_copy(s_buf.at[here], s_buf.at[here], s_recv.at[here]).wait()
         rows = pl.ds(pl.multiple_of(low * 32, 32), 32)
         f_buf[here] = (both[w, rows, :] + s_buf[here].astype(F32)).astype(BF16)
@@ -423,11 +423,9 @@
     pltpu.make_async_copy(recv.at[pl.ds(0, 31)], recv.at[pl.ds(0, 31)], a_send).wait()
     pltpu.make_async_copy(t_all.at[pl.ds(0, 3)], t_all.at[pl.ds(0, 3)], t_send).wait()
     pltpu.make_async_copy(half_times, half_times, u_send).wait()
-    for n in range(1, 16):
-        pltpu.make_async_copy(m_g.at[0], m_g.at[0], g_send.at[n]).wait()
-        pltpu.make_async_copy(m_h.at[0], m_h.at[0], h_send.at[n]).wait()
-    for n in range(8):
-        pltpu.make_async_copy(c_send.at[n], c_send.at[n], x_send.at[n]).wait()
+    pltpu.make_async_copy(g_all.at[pl.ds(0, 15)], g_all.at[pl.ds(0, 15)], g_send).wait()
+    pltpu.make_async_copy(h_all.at[pl.ds(0, 15)], h_all.at[pl.ds(0, 15)], h_send).wait()
+    pltpu.make_async_copy(c_send, c_send, x_send).wait()
     pltpu.make_async_copy(s_buf, s_buf, s_send).wait()
     final.wait()
     pltpu.make_async_copy(f_buf.at[pl.ds(0, 15)], f_buf.at[pl.ds(0, 15)], r_send).wait()
@@ -475,10 +473,10 @@
             pltpu.VMEM((16, 32, 256), BF16),
             pltpu.VMEM((16, 32, 256), BF16),
             pltpu.VMEM((16, 32, 256), BF16),
-            dma((32,)), dma, dma, dma, dma, dma,
-            dma((16,)), dma((16,)), dma((16,)), dma((16,)),
-            dma((7,)),
-            dma((8,)), dma((8,)),
+            dma((8,)), dma, dma, dma, dma, dma,
+            dma((16,)), dma, dma((16,)), dma,
+            dma((3,)),
+            dma((8,)), dma,
             dma((16,)), dma,
             dma, dma,
         ],

time: 50.3 us -> 47.7 us (0.948)
  Pallas kernels: 48.9 us -> 46.1 us
    pallas_call x1, Pallas kernels: 48.9 us -> 46.1 us  [local(): pl.pallas_call(kernel, out_shape=jax.ShapeDtypeStruct((27, 1, NG), F32),...]
where the time goes in v4:
time: 47.7 us; the launch traced here: 47.4 us
  Pallas kernels  46.1 us (97%)
  between operations  0.66 us (1%)
  local copies, waits for them, and re-layouts  0.64 us (1%)
    pallas_call x1, Pallas kernels, local(): pl.pallas_call(kernel, out_shape=jax.ShapeDtypeStruct((27, 1, NG), F32),...  46.1 us

profile of v4, /device:TPU:6, one launch (start us, length us, event | category | flops | bytes accessed | tf_op | source)
XLA Modules:
  0.0 47.4 jit_solution(2881147087931255605)
XLA Ops:
  0.7 46.1 %shard_map.73 = f32[27,1,864]{2,1,0:T(1,128)S(1)} custom-call(bf16[320,432]{1,0:T(8,128)(2,1)} %bitcast.3, f32[320]{0:T(512)} %gaps_hbm.1, f32[1]{0:T(128)S(6)} %copy.9.times_hbm, f32[8,8]{1,0:T(8,128)} %cw_hbm.1, f32[104,1024]{1,0:T(8,128)} %constant.6.clone.fac_hbm, s32[4,1024]{1,0:T(4,128)} %constant.7.clone.col_hbm, s32[1,512]{1,0:T(1,128)} %constant.8.clone.pts_hbm), custom_call_target="tpu_custom_call" | custom-call | tf_op jit(solution)/shard_map/pallas_call | solution.py:438
  46.8 0.6 %copy.10 = f32[1,27,864]{2,0,1:T(1,128)} copy(f32[1,27,864]{2,0,1:T(1,128)S(1)} %bitcast.2) | data formatting | bytes 186624

commit v5 on v4

--- a/solution.py
+++ b/solution.py
@@ -71,6 +71,7 @@
     (3, 1), (0, 2), (2, 0), (1, 2), (2, 1), (3, 2), (2, 3), (2, 2),
 )
 SLOT = {offset: n for n, offset in enumerate(OFFSETS)}
+MIRROR = [SLOT[dy, dx] for dx, dy in OFFSETS]
 FX, FXS, FY, FYS, FZ, FZS, FT = 0, 8, 16, 40, 64, 80, 96
 
 
@@ -79,7 +80,7 @@
     out_ref, gaps_ref, times_ref, cw_ref, col_ref, pts_ref, orb_ref, fac_ref,
     orb_p, recv, t_own, t_all, lead, quad, table, sel, acc, acc_odd, m_g, m_h, g_all, h_all,
     g_t, dmat, both, keep, c_send, c_recv, q_buf, s_buf, f_buf, r_buf,
-    a_recv, a_send, t_recv, t_send, u_recv, u_send, g_recv, g_send, h_recv, h_send, l_sem, x_recv, x_send, s_recv, s_send, r_recv, r_send,
+    a_recv, a_send, e_send, t_recv, t_send, u_recv, u_send, b_recv, g_send, h_send, l_sem, x_recv, x_send, s_recv, s_send, r_recv, r_send,
 ):
     tm = lax.axis_index("tm")
     sp = lax.axis_index("space")
@@ -144,12 +145,15 @@
         for part, block in enumerate(blocks):
             src, dst = orb_p.at[block], recv.at[sp, part]
             copy = remote(src, dst, a_send, a_recv.at[sp % 8], device(x, yy, zz, cc))
+            local = pltpu.make_async_copy(src, dst, a_recv.at[sp % 8])
             if dz == 0 and dy == 0:
-                local = pltpu.make_async_copy(src, dst, a_recv.at[sp % 8])
                 pl.when(core == cc)(local.start)
-                pl.when(core != cc)(copy.start)
+                if part == 0:
+                    pl.when(core != cc)(copy.start)
+            elif part == 0:
+                copy.start()
             else:
-                copy.start()
+                pl.when(core == cc)(copy.start)
     for load in loads:
         load.wait()
     t_own[...] = jnp.full((8, 128), times_ref[0], F32)
@@ -217,10 +221,14 @@
     acc_odd[...] = jnp.zeros_like(acc_odd)
 
     def chunk_step(step, carry):
-        turn = step // 2
+        turn = step // 4 * 2 + step % 2
         away = jnp.where(turn < 2, 2 * turn + 1, 6 - 2 * turn)
-        n = (y + away) % 4 * 2 + step % 2
+        passed = step // 2 % 2
+        n = (y + away) % 4 * 2 + (core + passed) % 2
         pltpu.make_async_copy(recv.at[pl.ds(0, 4)], recv.at[pl.ds(0, 4)], a_recv.at[n]).wait()
+        for quarter in range(4):
+            block = recv.at[n + 8 * quarter, 1]
+            pl.when(passed == 0)(remote(block, block, e_send, a_recv.at[n], device(x, y, z, 1 - core)).start)
         occupied = [recv[n + 8 * quarter, 0].astype(F32) for quarter in range(4)]
         empty = [recv[n + 8 * quarter, 1].astype(F32) for quarter in range(4)]
         minus, plus = ([], [], [], []), ([], [], [], [])
@@ -259,20 +267,20 @@
 
     def send_g(src, to, dx, dy):
         target = device((x + dx) % 4, (y + dy) % 4, z, core)
-        remote(src, g_all.at[to], g_send, g_recv.at[to], target).start()
+        remote(src, g_all.at[to], g_send, b_recv.at[to], target).start()
 
     def send_h(src, to, dx, dy):
         target = device((x + dx) % 4, (y + dy) % 4, z, core)
-        remote(src, h_all.at[to], h_send, h_recv.at[to], target).start()
+        remote(src, h_all.at[to], h_send, b_recv.at[MIRROR[to]], target).start()
 
     for d in (2, 1, 3):
         send_g(m_g.at[(y + d) % 4], SLOT[0, 4 - d], 0, d)
         send_h(m_h.at[(x + d) % 4], SLOT[4 - d, 0], d, 0)
-    for d in (1, 3):
+    for d in (2, 1, 3):
         send_g(m_g.at[y], SLOT[4 - d, 0], d, 0)
         send_h(m_h.at[x], SLOT[0, 4 - d], 0, d)
-    pltpu.make_async_copy(m_g.at[y], g_all.at[0], g_recv.at[0]).start()
-    pltpu.make_async_copy(m_h.at[x], h_all.at[0], h_recv.at[0]).start()
+    pltpu.make_async_copy(m_g.at[y], g_all.at[0], b_recv.at[0]).start()
+    pltpu.make_async_copy(m_h.at[x], h_all.at[0], b_recv.at[0]).start()
 
     pltpu.make_async_copy(half_times, half_times, u_recv).wait()
     pair_index = lax.broadcasted_iota(jnp.int32, (1, 1024), 1)
@@ -293,40 +301,29 @@
     decay = jnp.exp(-gap_i * tcol) * jnp.exp(-gap_a * tcol) * (NOCC**-0.5 * NEMP**-0.5)
     dmat[...] = jnp.dot(cw_ref[...], decay, precision=high, preferred_element_type=F32)
 
-    def arrived(buf, sem, slot):
-        pltpu.make_async_copy(buf.at[slot], buf.at[slot], sem.at[slot]).wait()
-
-    def got_g(dx, dy):
-        arrived(g_all, g_recv, SLOT[dx, dy])
-
-    def got_h(dx, dy):
-        arrived(h_all, h_recv, SLOT[dx, dy])
+    def got(dx, dy):
+        pltpu.make_async_copy(g_all.at[pl.ds(0, 2)], g_all.at[pl.ds(0, 2)], b_recv.at[SLOT[dx, dy]]).wait()
 
     def relay(d):
-        got_g(3, d)
-        up = (y + d) % 4 < 2
-        pl.when(up)(lambda: send_g(g_all.at[SLOT[3, d]], SLOT[2, d], 1, 0))
-        got_g(1, d)
-        pl.when(jnp.logical_not(up))(lambda: send_g(g_all.at[SLOT[1, d]], SLOT[2, d], 3, 0))
-        got_h(d, 3)
-        up = (x + d) % 4 < 2
-        pl.when(up)(lambda: send_h(h_all.at[SLOT[d, 3]], SLOT[d, 2], 0, 1))
-        got_h(d, 1)
-        pl.when(jnp.logical_not(up))(lambda: send_h(h_all.at[SLOT[d, 1]], SLOT[d, 2], 0, 3))
-
-    relay(0)
+        up_g, up_h = (y + d) % 4 < 2, (x + d) % 4 < 2
+        got(3, d)
+        pl.when(up_g)(lambda: send_g(g_all.at[SLOT[3, d]], SLOT[2, d], 1, 0))
+        pl.when(up_h)(lambda: send_h(h_all.at[SLOT[d, 3]], SLOT[d, 2], 0, 1))
+        got(1, d)
+        pl.when(jnp.logical_not(up_g))(lambda: send_g(g_all.at[SLOT[1, d]], SLOT[2, d], 3, 0))
+        pl.when(jnp.logical_not(up_h))(lambda: send_h(h_all.at[SLOT[d, 1]], SLOT[d, 2], 0, 3))
+
     for d in (1, 3, 2):
-        got_g(0, d)
+        got(0, d)
         send_g(g_all.at[SLOT[0, d]], SLOT[3, d], 1, 0)
         send_g(g_all.at[SLOT[0, d]], SLOT[1, d], 3, 0)
-        got_h(d, 0)
         send_h(h_all.at[SLOT[d, 0]], SLOT[d, 3], 0, 1)
         send_h(h_all.at[SLOT[d, 0]], SLOT[d, 1], 0, 3)
     relay(1)
     relay(3)
     relay(2)
-    got_g(0, 0)
-    got_h(0, 0)
+    for d in (0, 1, 3):
+        got(d, 0)
 
     def turn_g(start):
         for n in range(start, start + 4):
@@ -343,8 +340,7 @@
 
     lax.fori_loop(0, 8, early, 0)
     for d in range(4):
-        got_g(2, d)
-        got_h(d, 2)
+        got(2, d)
     turn_g(4)
     sibling = device(x, y, z, 1 - core)
     mine = pl.ds(pl.multiple_of(core * 128, 128), 128)
@@ -366,7 +362,7 @@
         for m in range(2):
             w = first + m
             c_send[w] = (keep[w, other, :] + total[m * 128 : (m + 1) * 128, :]).astype(BF16)
-            remote(c_send.at[w], c_recv.at[w], x_send, x_recv.at[w], sibling).start()
+            remote(c_send.at[w], c_recv.at[w], x_send, x_recv.at[n], sibling).start()
         return carry
 
     def both_cores(n, carry):
@@ -374,7 +370,9 @@
         rest = late(first, mine)
         for m in range(2):
             w = first + m
-            pltpu.make_async_copy(c_recv.at[w], c_recv.at[w], x_recv.at[w]).wait()
+            if m == 0:
+                two = c_recv.at[pl.ds(0, 2)]
+                pltpu.make_async_copy(two, two, x_recv.at[n]).wait()
             total = keep[w, mine, :] + rest[m * 128 : (m + 1) * 128, :] + c_recv[w].astype(F32)
             both[w] = total
             for low in range(4):
@@ -420,7 +418,8 @@
     final = pltpu.make_async_copy(out_ref, out_any, l_sem.at[0])
     final.start()
 
-    pltpu.make_async_copy(recv.at[pl.ds(0, 31)], recv.at[pl.ds(0, 31)], a_send).wait()
+    pltpu.make_async_copy(recv.at[pl.ds(0, 23)], recv.at[pl.ds(0, 23)], a_send).wait()
+    pltpu.make_async_copy(recv.at[pl.ds(0, 8)], recv.at[pl.ds(0, 8)], e_send).wait()
     pltpu.make_async_copy(t_all.at[pl.ds(0, 3)], t_all.at[pl.ds(0, 3)], t_send).wait()
     pltpu.make_async_copy(half_times, half_times, u_send).wait()
     pltpu.make_async_copy(g_all.at[pl.ds(0, 15)], g_all.at[pl.ds(0, 15)], g_send).wait()
@@ -473,10 +472,10 @@
             pltpu.VMEM((16, 32, 256), BF16),
             pltpu.VMEM((16, 32, 256), BF16),
             pltpu.VMEM((16, 32, 256), BF16),
-            dma((8,)), dma, dma, dma, dma, dma,
-            dma((16,)), dma, dma((16,)), dma,
+            dma((8,)), dma, dma, dma, dma, dma, dma,
+            dma((16,)), dma, dma,
             dma((3,)),
-            dma((8,)), dma,
+            dma((4,)), dma,
             dma((16,)), dma,
             dma, dma,
         ],

time: 47.7 us -> 46.4 us (0.973)
  Pallas kernels: 46.1 us -> 44.7 us
    pallas_call x1, Pallas kernels: 46.1 us -> 44.7 us  [local(): pl.pallas_call(kernel, out_shape=jax.ShapeDtypeStruct((27, 1, NG), F32),...]
where the time goes in v5:
time: 46.4 us; the launch traced here: 46 us
  Pallas kernels  44.7 us (96%)
  between operations  0.66 us (1%)
  local copies, waits for them, and re-layouts  0.64 us (1%)
    pallas_call x1, Pallas kernels, local(): pl.pallas_call(kernel, out_shape=jax.ShapeDtypeStruct((27, 1, NG), F32),...  44.7 us

profile of v5, /device:TPU:6, one launch (start us, length us, event | category | flops | bytes accessed | tf_op | source)
XLA Modules:
  0.0 46.0 jit_solution(6903688206749204048)
XLA Ops:
  0.7 44.7 %shard_map.73 = f32[27,1,864]{2,1,0:T(1,128)S(1)} custom-call(bf16[320,432]{1,0:T(8,128)(2,1)} %bitcast.3, f32[320]{0:T(512)} %gaps_hbm.1, f32[1]{0:T(128)S(6)} %copy.9.times_hbm, f32[8,8]{1,0:T(8,128)} %cw_hbm.1, f32[104,1024]{1,0:T(8,128)} %constant.6.clone.fac_hbm, s32[4,1024]{1,0:T(4,128)} %constant.7.clone.col_hbm, s32[1,512]{1,0:T(1,128)} %constant.8.clone.pts_hbm), custom_call_target="tpu_custom_call" | custom-call | tf_op jit(solution)/shard_map/pallas_call | solution.py:437
  45.3 0.6 %copy.10 = f32[1,27,864]{2,0,1:T(1,128)} copy(f32[1,27,864]{2,0,1:T(1,128)S(1)} %bitcast.2) | data formatting | bytes 186624

commit v6 on v5

--- a/solution.py
+++ b/solution.py
@@ -116,6 +116,7 @@
         pl.semaphore_signal(barrier, inc=1, device_id=target, device_id_type=MESH)
 
     far = (z + 6 + 4 * core) % 8
+    greet(device(x, y, (z + 4) % 8, core))
     for dy in (2, 1, 3, 0):
         yy = (y + dy) % 4
         for cc in range(2):
@@ -127,7 +128,6 @@
         greet(device(x, yy, z, 1 - core))
     for dx in range(1, 4):
         greet(device((x + dx) % 4, y, z, core))
-    greet(device(x, y, (z + 4) % 8, core))
 
     load_pts.wait()
     pick = lax.broadcasted_iota(jnp.int32, (432, 512), 0) == pts_ref[...]
@@ -262,25 +262,28 @@
     m_all = jnp.concatenate(columns, axis=1).astype(BF16)
     for n in range(4):
         lanes = slice(n * 256, (n + 1) * 256)
-        m_g[n] = jnp.dot(m_all, sel[0, :, lanes], preferred_element_type=F32).astype(BF16)
-        m_h[n] = jnp.dot(m_all, sel[1, :, lanes], preferred_element_type=F32).astype(BF16)
-
-    def send_g(src, to, dx, dy):
+        m_g[n] = jnp.dot(m_all, sel[0, :, lanes], preferred_element_type=F32).astype(BF16).reshape(2, 32, 256)
+        m_h[n] = jnp.dot(m_all, sel[1, :, lanes], preferred_element_type=F32).astype(BF16).reshape(2, 32, 256)
+
+    def send_g(src, to, dx, dy, half):
         target = device((x + dx) % 4, (y + dy) % 4, z, core)
-        remote(src, g_all.at[to], g_send, b_recv.at[to], target).start()
-
-    def send_h(src, to, dx, dy):
+        remote(src.at[half], g_all.at[to, half], g_send, b_recv.at[to, half], target).start()
+
+    def send_h(src, to, dx, dy, half):
         target = device((x + dx) % 4, (y + dy) % 4, z, core)
-        remote(src, h_all.at[to], h_send, b_recv.at[MIRROR[to]], target).start()
-
-    for d in (2, 1, 3):
-        send_g(m_g.at[(y + d) % 4], SLOT[0, 4 - d], 0, d)
-        send_h(m_h.at[(x + d) % 4], SLOT[4 - d, 0], d, 0)
-    for d in (2, 1, 3):
-        send_g(m_g.at[y], SLOT[4 - d, 0], d, 0)
-        send_h(m_h.at[x], SLOT[0, 4 - d], 0, d)
-    pltpu.make_async_copy(m_g.at[y], g_all.at[0], b_recv.at[0]).start()
-    pltpu.make_async_copy(m_h.at[x], h_all.at[0], b_recv.at[0]).start()
+        remote(src.at[half], h_all.at[to, half], h_send, b_recv.at[MIRROR[to], half], target).start()
+
+    for half in range(2):
+        for d in (2, 1, 3):
+            send_g(m_g.at[(y + d) % 4], SLOT[0, 4 - d], 0, d, half)
+            send_h(m_h.at[(x + d) % 4], SLOT[4 - d, 0], d, 0, half)
+    for half in range(2):
+        for d in (1, 3, 2):
+            send_g(m_g.at[y], SLOT[4 - d, 0], d, 0, half)
+            send_h(m_h.at[x], SLOT[0, 4 - d], 0, d, half)
+    for half in range(2):
+        pltpu.make_async_copy(m_g.at[y, half], g_all.at[0, half], b_recv.at[0, half]).start()
+        pltpu.make_async_copy(m_h.at[x, half], h_all.at[0, half], b_recv.at[0, half]).start()
 
     pltpu.make_async_copy(half_times, half_times, u_recv).wait()
     pair_index = lax.broadcasted_iota(jnp.int32, (1, 1024), 1)
@@ -301,33 +304,34 @@
     decay = jnp.exp(-gap_i * tcol) * jnp.exp(-gap_a * tcol) * (NOCC**-0.5 * NEMP**-0.5)
     dmat[...] = jnp.dot(cw_ref[...], decay, precision=high, preferred_element_type=F32)
 
-    def got(dx, dy):
-        pltpu.make_async_copy(g_all.at[pl.ds(0, 2)], g_all.at[pl.ds(0, 2)], b_recv.at[SLOT[dx, dy]]).wait()
-
-    def relay(d):
+    def got(dx, dy, half):
+        pltpu.make_async_copy(g_all.at[0], g_all.at[0], b_recv.at[SLOT[dx, dy], half]).wait()
+
+    def relay(d, half):
         up_g, up_h = (y + d) % 4 < 2, (x + d) % 4 < 2
-        got(3, d)
-        pl.when(up_g)(lambda: send_g(g_all.at[SLOT[3, d]], SLOT[2, d], 1, 0))
-        pl.when(up_h)(lambda: send_h(h_all.at[SLOT[d, 3]], SLOT[d, 2], 0, 1))
-        got(1, d)
-        pl.when(jnp.logical_not(up_g))(lambda: send_g(g_all.at[SLOT[1, d]], SLOT[2, d], 3, 0))
-        pl.when(jnp.logical_not(up_h))(lambda: send_h(h_all.at[SLOT[d, 1]], SLOT[d, 2], 0, 3))
-
+        got(3, d, half)
+        pl.when(up_g)(lambda: send_g(g_all.at[SLOT[3, d]], SLOT[2, d], 1, 0, half))
+        pl.when(up_h)(lambda: send_h(h_all.at[SLOT[d, 3]], SLOT[d, 2], 0, 1, half))
+        got(1, d, half)
+        pl.when(jnp.logical_not(up_g))(lambda: send_g(g_all.at[SLOT[1, d]], SLOT[2, d], 3, 0, half))
+        pl.when(jnp.logical_not(up_h))(lambda: send_h(h_all.at[SLOT[d, 1]], SLOT[d, 2], 0, 3, half))
+
+    for d, half in ((1, 0), (3, 0), (2, 0), (1, 1), (3, 1), (2, 1)):
+        got(0, d, half)
+        send_g(g_all.at[SLOT[0, d]], SLOT[3, d], 1, 0, half)
+        send_g(g_all.at[SLOT[0, d]], SLOT[1, d], 3, 0, half)
+        send_h(h_all.at[SLOT[d, 0]], SLOT[d, 3], 0, 1, half)
+        send_h(h_all.at[SLOT[d, 0]], SLOT[d, 1], 0, 3, half)
     for d in (1, 3, 2):
-        got(0, d)
-        send_g(g_all.at[SLOT[0, d]], SLOT[3, d], 1, 0)
-        send_g(g_all.at[SLOT[0, d]], SLOT[1, d], 3, 0)
-        send_h(h_all.at[SLOT[d, 0]], SLOT[d, 3], 0, 1)
-        send_h(h_all.at[SLOT[d, 0]], SLOT[d, 1], 0, 3)
-    relay(1)
-    relay(3)
-    relay(2)
+        for half in range(2):
+            relay(d, half)
     for d in (0, 1, 3):
-        got(d, 0)
+        for half in range(2):
+            got(d, 0, half)
 
     def turn_g(start):
         for n in range(start, start + 4):
-            block = jnp.concatenate([g_all[2 * n], g_all[2 * n + 1]], axis=0).astype(F32)
+            block = g_all[2 * n : 2 * n + 2].reshape(128, 256).astype(F32)
             g_t[:, n * 128 : (n + 1) * 128] = block.T
 
     turn_g(0)
@@ -340,7 +344,8 @@
 
     lax.fori_loop(0, 8, early, 0)
     for d in range(4):
-        got(2, d)
+        for half in range(2):
+            got(2, d, half)
     turn_g(4)
     sibling = device(x, y, z, 1 - core)
     mine = pl.ds(pl.multiple_of(core * 128, 128), 128)
@@ -356,8 +361,11 @@
         left = jnp.concatenate(left, axis=0).astype(BF16)
         return jnp.dot(left, h_late, preferred_element_type=F32)
 
+    def pair_of(n):
+        return (x + jnp.where(n == 0, 1, jnp.where(n == 1, 3, jnp.where(n == 2, 2, 0)))) % 4
+
     def for_sibling(n, carry):
-        first = 2 * n
+        first = 2 * pair_of(n)
         total = late(first, other)
         for m in range(2):
             w = first + m
@@ -366,7 +374,7 @@
         return carry
 
     def both_cores(n, carry):
-        first = 2 * n
+        first = 2 * pair_of(n)
         rest = late(first, mine)
         for m in range(2):
             w = first + m
@@ -392,7 +400,7 @@
     def deliver(n, carry):
         step = 3 - n % 4
         owner = (z + side * step + 8) % 8
-        pair = n // 4
+        pair = pair_of(n // 4)
         w, low = pair * 2 + owner // 4, owner % 4
         here = pair * 4 + step
         pltpu.make_async_copy(s_buf.at[here], s_buf.at[here], s_recv.at[here]).wait()
@@ -458,10 +466,10 @@
             pltpu.VMEM((2, 1024, 1024), BF16),
             pltpu.VMEM((64, 512), F32),
             pltpu.VMEM((128, 512), F32),
-            pltpu.VMEM((4, 64, 256), BF16),
-            pltpu.VMEM((4, 64, 256), BF16),
-            pltpu.VMEM((16, 64, 256), BF16),
-            pltpu.VMEM((16, 64, 256), BF16),
+            pltpu.VMEM((4, 2, 32, 256), BF16),
+            pltpu.VMEM((4, 2, 32, 256), BF16),
+            pltpu.VMEM((16, 2, 32, 256), BF16),
+            pltpu.VMEM((16, 2, 32, 256), BF16),
             pltpu.VMEM((256, 1024), F32),
             pltpu.VMEM((8, 1024), F32),
             pltpu.VMEM((8, 128, 256), F32),
@@ -473,7 +481,7 @@
             pltpu.VMEM((16, 32, 256), BF16),
             pltpu.VMEM((16, 32, 256), BF16),
             dma((8,)), dma, dma, dma, dma, dma, dma,
-            dma((16,)), dma, dma,
+            dma((16, 2)), dma, dma,
             dma((3,)),
             dma((4,)), dma,
             dma((16,)), dma,

time: 46.4 us -> 45.9 us (0.989); the launches traced: 46 us -> 45 us
  Pallas kernels: 44.7 us -> 43.7 us
    pallas_call x1, Pallas kernels: 44.7 us -> 43.7 us  [local(): pl.pallas_call(kernel, out_shape=jax.ShapeDtypeStruct((27, 1, NG), F32),...]
where the time goes in v6:
time: 45.9 us; the launch traced here: 45 us
  Pallas kernels  43.7 us (95%)
  between operations  0.66 us (1%)
  local copies, waits for them, and re-layouts  0.64 us (1%)
    pallas_call x1, Pallas kernels, local(): pl.pallas_call(kernel, out_shape=jax.ShapeDtypeStruct((27, 1, NG), F32),...  43.7 us

profile of v6, /device:TPU:6, one launch (start us, length us, event | category | flops | bytes accessed | tf_op | source)
XLA Modules:
  0.0 45.0 jit_solution(2354164014748499248)
XLA Ops:
  0.7 43.7 %shard_map.73 = f32[27,1,864]{2,1,0:T(1,128)S(1)} custom-call(bf16[320,432]{1,0:T(8,128)(2,1)} %bitcast.3, f32[320]{0:T(512)} %gaps_hbm.1, f32[1]{0:T(128)S(6)} %copy.9.times_hbm, f32[8,8]{1,0:T(8,128)} %cw_hbm.1, f32[104,1024]{1,0:T(8,128)} %constant.6.clone.fac_hbm, s32[4,1024]{1,0:T(4,128)} %constant.7.clone.col_hbm, s32[1,512]{1,0:T(1,128)} %constant.8.clone.pts_hbm), custom_call_target="tpu_custom_call" | custom-call | tf_op jit(solution)/shard_map/pallas_call | solution.py:445
  44.3 0.6 %copy.10 = f32[1,27,864]{2,0,1:T(1,128)} copy(f32[1,27,864]{2,0,1:T(1,128)S(1)} %bitcast.2) | data formatting | bytes 186624

commit v7 on v6

--- a/solution.py
+++ b/solution.py
@@ -118,14 +118,16 @@
     far = (z + 6 + 4 * core) % 8
     greet(device(x, y, (z + 4) % 8, core))
     for dy in (2, 1, 3, 0):
-        yy = (y + dy) % 4
         for cc in range(2):
-            greet(device(x, yy, far, cc))
-            greet(device(x, yy, (z + 1) % 8, cc))
-            greet(device(x, yy, (z + 7) % 8, cc))
+            greet(device(x, (y + dy) % 4, far, cc))
+    for dy in (2, 1, 3, 0):
+        for cc in range(2):
+            greet(device(x, (y + dy) % 4, (z + 1) % 8, cc))
+            greet(device(x, (y + dy) % 4, (z + 7) % 8, cc))
+    for dy in (2, 1, 3, 0):
         if dy > 0:
-            greet(device(x, yy, z, core))
-        greet(device(x, yy, z, 1 - core))
+            greet(device(x, (y + dy) % 4, z, core))
+        greet(device(x, (y + dy) % 4, z, 1 - core))
     for dx in range(1, 4):
         greet(device((x + dx) % 4, y, z, core))
 
@@ -373,6 +375,10 @@
             remote(c_send.at[w], c_recv.at[w], x_send, x_recv.at[n], sibling).start()
         return carry
 
+    def either(action):
+        pl.when(x < 3)(lambda: action(slice(0, 256)))
+        pl.when(x == 3)(lambda: action(slice(0, 128)))
+
     def both_cores(n, carry):
         first = 2 * pair_of(n)
         rest = late(first, mine)
@@ -385,12 +391,17 @@
             both[w] = total
             for low in range(4):
                 q_buf[w * 4 + low] = total[low * 32 : (low + 1) * 32, :].astype(BF16)
-            for low in range(4):
-                owner = m * 4 + low
-                step = ((owner - z) * side + 8) % 8
-                there = first * 2 + 7 - step
-                copy = remote(q_buf.at[w * 4 + low], s_buf.at[there], s_send, s_recv.at[there], partner)
-                pl.when(step >= 4)(copy.start)
+            for step in range(4, 8):
+                owner = (z + side * step + 8) % 8
+                there = w // 2 * 4 + 7 - step
+                src, dst = q_buf.at[w * 4 + owner % 4], s_buf.at[there]
+
+                def exchange():
+                    either(lambda lanes: remote(
+                        src.at[:, lanes], dst.at[:, lanes], s_send, s_recv.at[there], partner
+                    ).start())
+
+                pl.when(owner // 4 == m)(exchange)
         return carry
 
     lax.fori_loop(0, 4, for_sibling, 0)
@@ -398,24 +409,35 @@
     slot = (z + core) // 2 % 4 * 4 + x
 
     def deliver(n, carry):
-        step = 3 - n % 4
-        owner = (z + side * step + 8) % 8
-        pair = pair_of(n // 4)
-        w, low = pair * 2 + owner // 4, owner % 4
-        here = pair * 4 + step
-        pltpu.make_async_copy(s_buf.at[here], s_buf.at[here], s_recv.at[here]).wait()
-        rows = pl.ds(pl.multiple_of(low * 32, 32), 32)
-        f_buf[here] = (both[w, rows, :] + s_buf[here].astype(F32)).astype(BF16)
-        target = low * 8 + y * 2 + core
-        copy = remote(f_buf.at[here], r_buf.at[slot], r_send, r_recv, (w, target))
-        local = pltpu.make_async_copy(f_buf.at[here], r_buf.at[slot], r_recv)
-        own_block = jnp.logical_and(w == tm, target == sp)
-        pl.when(own_block)(local.start)
-        pl.when(jnp.logical_not(own_block))(copy.start)
-        return carry
-
-    lax.fori_loop(0, 16, deliver, 0)
-    pltpu.make_async_copy(r_buf, r_buf, r_recv).wait()
+        w = 2 * pair_of(n // 2) + n % 2
+        for step in (3, 2, 1, 0):
+            owner = (z + side * step + 8) % 8
+            low, here = owner % 4, w // 2 * 4 + step
+
+            def send():
+                held = s_buf.at[here]
+                either(lambda lanes: pltpu.make_async_copy(held.at[:, lanes], held.at[:, lanes], s_recv.at[here]).wait())
+                rows = pl.ds(pl.multiple_of(low * 32, 32), 32)
+                f_buf[here] = (both[w, rows, :] + s_buf[here].astype(F32)).astype(BF16)
+                own_block = jnp.logical_and(w == tm, step == 0)
+                src, dst = f_buf.at[here], r_buf.at[slot]
+
+                def pass_on():
+                    either(lambda lanes: remote(
+                        src.at[:, lanes], dst.at[:, lanes], r_send, r_recv, (w, low * 8 + y * 2 + core)
+                    ).start())
+
+                def take():
+                    either(lambda lanes: pltpu.make_async_copy(src.at[:, lanes], dst.at[:, lanes], r_recv).start())
+
+                pl.when(own_block)(take)
+                pl.when(jnp.logical_not(own_block))(pass_on)
+
+            pl.when(owner // 4 == n % 2)(send)
+        return carry
+
+    lax.fori_loop(0, 8, deliver, 0)
+    pltpu.make_async_copy(r_buf.at[pl.ds(0, 14)], r_buf.at[pl.ds(0, 14)], r_recv).wait()
     for n in range(4):
         total = r_buf[n].astype(F32)
         for m in range(1, 4):
@@ -433,9 +455,10 @@
     pltpu.make_async_copy(g_all.at[pl.ds(0, 15)], g_all.at[pl.ds(0, 15)], g_send).wait()
     pltpu.make_async_copy(h_all.at[pl.ds(0, 15)], h_all.at[pl.ds(0, 15)], h_send).wait()
     pltpu.make_async_copy(c_send, c_send, x_send).wait()
-    pltpu.make_async_copy(s_buf, s_buf, s_send).wait()
+    either(lambda lanes: pltpu.make_async_copy(s_buf.at[:, :, lanes], s_buf.at[:, :, lanes], s_send).wait())
     final.wait()
-    pltpu.make_async_copy(f_buf.at[pl.ds(0, 15)], f_buf.at[pl.ds(0, 15)], r_send).wait()
+    sent = f_buf.at[pl.ds(0, 15)]
+    either(lambda lanes: pltpu.make_async_copy(sent.at[:, :, lanes], sent.at[:, :, lanes], r_send).wait())
 
 
 def local(orbitals, gaps, times, cos_weights):

time: 45.9 us -> 45.4 us (0.989)
  the two profiles are of different devices: /device:TPU:6 before, /device:TPU:1 now
where the time goes in v7:
time: 45.4 us; the launch traced here: 45.3 us
  Pallas kernels  44 us (97%)
  between operations  0.66 us (1%)
  local copies, waits for them, and re-layouts  0.64 us (1%)
    pallas_call x1, Pallas kernels, local(): pl.pallas_call(kernel, out_shape=jax.ShapeDtypeStruct((27, 1, NG), F32),...  44 us

profile of v7, /device:TPU:1, one launch (start us, length us, event | category | flops | bytes accessed | tf_op | source)
XLA Modules:
  0.0 45.3 jit_solution(4252129495560150082)
XLA Ops:
  0.7 44.0 %shard_map.73 = f32[27,1,864]{2,1,0:T(1,128)S(1)} custom-call(bf16[320,432]{1,0:T(8,128)(2,1)} %bitcast.3, f32[320]{0:T(512)} %gaps_hbm.1, f32[1]{0:T(128)S(6)} %copy.9.times_hbm, f32[8,8]{1,0:T(8,128)} %cw_hbm.1, f32[104,1024]{1,0:T(8,128)} %constant.6.clone.fac_hbm, s32[4,1024]{1,0:T(4,128)} %constant.7.clone.col_hbm, s32[1,512]{1,0:T(1,128)} %constant.8.clone.pts_hbm), custom_call_target="tpu_custom_call" | custom-call | tf_op jit(solution)/shard_map/pallas_call | solution.py:468
  44.7 0.6 %copy.10 = f32[1,27,864]{2,0,1:T(1,128)} copy(f32[1,27,864]{2,0,1:T(1,128)S(1)} %bitcast.2) | data formatting | bytes 186624

commit v8 on v7

--- a/solution.py
+++ b/solution.py
@@ -76,8 +76,8 @@
 
 
 def kernel(
-    orb_hbm, gaps_hbm, times_hbm, cw_hbm, fac_hbm, col_hbm, pts_hbm, out_any,
-    out_ref, gaps_ref, times_ref, cw_ref, col_ref, pts_ref, orb_ref, fac_ref,
+    orb_hbm, gaps_hbm, times_hbm, cw_hbm, fac_hbm, col_hbm, pts_hbm, out_ref,
+    gaps_ref, times_ref, cw_ref, col_ref, pts_ref, orb_ref, fac_ref,
     orb_p, recv, t_own, t_all, lead, quad, table, sel, acc, acc_odd, m_g, m_h, g_all, h_all,
     g_t, dmat, both, keep, c_send, c_recv, q_buf, s_buf, f_buf, r_buf,
     a_recv, a_send, e_send, t_recv, t_send, u_recv, u_send, b_recv, g_send, h_send, l_sem, x_recv, x_send, s_recv, s_send, r_recv, r_send,
@@ -445,9 +445,6 @@
         width = 256 if n < 3 else 96
         out_ref[:, 0, n * 256 : n * 256 + width] = total[:27, :width]
 
-    final = pltpu.make_async_copy(out_ref, out_any, l_sem.at[0])
-    final.start()
-
     pltpu.make_async_copy(recv.at[pl.ds(0, 23)], recv.at[pl.ds(0, 23)], a_send).wait()
     pltpu.make_async_copy(recv.at[pl.ds(0, 8)], recv.at[pl.ds(0, 8)], e_send).wait()
     pltpu.make_async_copy(t_all.at[pl.ds(0, 3)], t_all.at[pl.ds(0, 3)], t_send).wait()
@@ -456,7 +453,6 @@
     pltpu.make_async_copy(h_all.at[pl.ds(0, 15)], h_all.at[pl.ds(0, 15)], h_send).wait()
     pltpu.make_async_copy(c_send, c_send, x_send).wait()
     either(lambda lanes: pltpu.make_async_copy(s_buf.at[:, :, lanes], s_buf.at[:, :, lanes], s_send).wait())
-    final.wait()
     sent = f_buf.at[pl.ds(0, 15)]
     either(lambda lanes: pltpu.make_async_copy(sent.at[:, :, lanes], sent.at[:, :, lanes], r_send).wait())
 
@@ -469,9 +465,8 @@
         kernel,
         out_shape=jax.ShapeDtypeStruct((27, 1, NG), F32),
         in_specs=[pl.BlockSpec(memory_space=pltpu.HBM)] * 7,
-        out_specs=pl.BlockSpec(memory_space=pl.ANY),
+        out_specs=pl.BlockSpec(memory_space=pltpu.VMEM),
         scratch_shapes=[
-            pltpu.VMEM((27, 1, NG), F32),
             pltpu.VMEM((NOCC + NEMP,), F32),
             pltpu.SMEM((1,), F32),
             pltpu.VMEM((8, 8), F32),

time: 45.4 us -> 45.2 us (level)
  no operation moved by 1% of the time
where the time goes in v8:
time: 45.2 us; the launch traced here: 45.1 us
  Pallas kernels  43.8 us (97%)
  between operations  0.66 us (1%)
  local copies, waits for them, and re-layouts  0.64 us (1%)
    pallas_call x1, Pallas kernels, local(): pl.pallas_call(kernel, out_shape=jax.ShapeDtypeStruct((27, 1, NG), F32),...  43.8 us

profile of v8, /device:TPU:1, one launch (start us, length us, event | category | flops | bytes accessed | tf_op | source)
XLA Modules:
  0.0 45.1 jit_solution(10916136100643280727)
XLA Ops:
  0.7 43.8 %shard_map.73 = f32[27,1,864]{2,1,0:T(1,128)S(1)} custom-call(bf16[320,432]{1,0:T(8,128)(2,1)} %bitcast.3, f32[320]{0:T(512)} %gaps_hbm.1, f32[1]{0:T(128)S(6)} %copy.9.times_hbm, f32[8,8]{1,0:T(8,128)} %cw_hbm.1, f32[104,1024]{1,0:T(8,128)} %constant.6.clone.fac_hbm, s32[4,1024]{1,0:T(4,128)} %constant.7.clone.col_hbm, s32[1,512]{1,0:T(1,128)} %constant.8.clone.pts_hbm), custom_call_target="tpu_custom_call" | custom-call | tf_op jit(solution)/shard_map/pallas_call | solution.py:464
  44.5 0.6 %copy.10 = f32[1,27,864]{2,0,1:T(1,128)} copy(f32[1,27,864]{2,0,1:T(1,128)S(1)} %bitcast.2) | data formatting | bytes 186624
